TPU v7x, 128 devices: a whole 4x4x4 slice. The times are simulated.
128 devices in a mesh: front: 4 (over z), blk: 32 (over x, y, core).
Axes of the slice: x: 4, y: 4, z: 4, core: 2. Of those that a mesh axis runs over, the one named last changes fastest.
Arguments:
- panel_column: bfloat16 [4, 16384, 256], P('front', 'blk'), may hold values from -6 to 6
- upper_inverse: bfloat16 [4, 256, 256], P('front'), may hold values from -0.375 to 0.375
- panel_rows: bfloat16 [4, 256, 12288], P('front', None, 'blk'), may hold values from -0.375 to 0.375
- trailing: bfloat16 [4, 16384, 12288], P('front', 'blk')
- sketch: bfloat16 [12288, 256], replicated, may hold values from -0.0546875 to 0.0546875
- row_map: int32 [4, 64, 256], P('front', 'blk'), may hold values from 0 to 255, each once within a row
- parent_block: int32 [4, 64], replicated, may hold values from 0 to 95, as said below
- parent_slot: int32 [96], replicated, may hold values from 0 to 127, as said below
Outputs:
- factored_column: bfloat16 [4, 16384, 256], P('front', 'blk')
- right_factor: bfloat16 [4, 12288, 256], P('front', 'blk')
- parent_left: bfloat16 [32768, 1024], P(('front', 'blk'))
Inputs may be any that keep to these rules, and one draw needn't show every extreme that they name: `parent_block`: within one front the 64 blocks go to distinct parent blocks; some parent block receives a block of every front. `parent_slot`: distinct values: a device owns at most one parent block.
All inputs are finite; a program needn't handle non-finite values.
Results may differ from a plain program's by a relative error of at most 0.0095.
Values may be sent and summed in bfloat16 or wider, within the bound.
A program may use at most 128 MiB of HBM per device.

v0:
```python
import math

import jax
import jax.numpy as jnp
from jax import lax
from jax.sharding import PartitionSpec as P


def gathered_total(x, axis):
    return lax.all_gather(x, axis).astype(jnp.float32).sum(0)


def gram_factor(sketched, slab_rows):
    local_gram = lax.dot_general(
        sketched, sketched, (((0,), (0,)), ((), ())), preferred_element_type=jnp.float32
    )
    gram_matrix = (
        gathered_total(local_gram.astype(jnp.bfloat16), "blk").astype(jnp.float32) / slab_rows
    )
    return jnp.linalg.cholesky(gram_matrix)


def body(
    panel_column, upper_inverse, panel_rows, trailing, sketch, row_map, parent_block, parent_slot
):
    blk_count = lax.axis_size("blk")
    front_count = lax.axis_size("front")
    front_index = lax.axis_index("front")
    block_index = lax.axis_index("blk")
    trail_local = trailing[0]
    local_rows = trail_local.shape[0]
    block_rows = row_map.shape[2]
    per_device = row_map.shape[1]
    rank_width = sketch.shape[1]
    slab_rows = local_rows * blk_count
    factored = jnp.dot(
        panel_column[0], upper_inverse[0], preferred_element_type=jnp.float32
    ).astype(jnp.bfloat16)
    window = trail_local.astype(jnp.float32)
    updated = (
        window
        - jnp.dot(
            factored,
            lax.all_gather(panel_rows, "blk", axis=2, tiled=True)[0],
            preferred_element_type=jnp.float32,
        )
    ).astype(jnp.bfloat16)
    sketched = jnp.dot(updated, sketch, preferred_element_type=jnp.float32).astype(jnp.bfloat16)
    factor_low = gram_factor(sketched, slab_rows)
    basis_rows = jax.scipy.linalg.solve_triangular(
        factor_low, sketched.astype(jnp.float32).T, lower=True
    ).T
    window = updated
    cross_share = lax.psum_scatter(
        lax.dot_general(
            window, sketched, (((0,), (0,)), ((), ())), preferred_element_type=jnp.float32
        ),
        "blk",
        scatter_dimension=0,
        tiled=True,
    )
    right_rows = jax.scipy.linalg.solve_triangular(
        factor_low, cross_share.T, lower=True
    ).T / math.sqrt(slab_rows)
    left_rows = basis_rows.astype(jnp.bfloat16).reshape(per_device, block_rows, rank_width)
    position = jnp.arange(block_rows, dtype=jnp.int32)
    permuter = (row_map[0][:, None, :] == position[None, :, None]).astype(jnp.bfloat16)
    placed = jnp.einsum(
        "bpr,brk->bpk", permuter, left_rows, preferred_element_type=jnp.float32
    ).astype(jnp.bfloat16)
    parent_count = parent_slot.shape[0]
    parent_number = jnp.arange(parent_count, dtype=jnp.int32)
    owner_all = jnp.sum(
        jnp.where(
            parent_block[:, :, None] == parent_number[None, None, :], parent_slot[None, None, :], 0
        ),
        axis=2,
    )
    block_total = owner_all.shape[1]
    all_blocks = lax.all_gather(placed, "blk", axis=0, tiled=True)
    own_owners = lax.dynamic_slice(owner_all, (front_index, 0), (1, block_total))[0]
    targets = jnp.arange(front_count, dtype=jnp.int32) * blk_count + block_index
    selector = (own_owners[None, :] == targets[:, None]).astype(jnp.bfloat16)
    outgoing = jnp.einsum(
        "gj,jxk->xgk", selector, all_blocks, preferred_element_type=jnp.float32
    ).astype(jnp.bfloat16)
    gathered = lax.all_to_all(outgoing, "front", split_axis=1, concat_axis=1, tiled=True)
    parent_rows = gathered.reshape(block_rows, front_count * rank_width)
    return (factored[None], right_rows.astype(jnp.bfloat16)[None], parent_rows)


def solution(mesh):
    return jax.shard_map(
        body,
        mesh=mesh,
        in_specs=(
            P("front", "blk", None),
            P("front", None, None),
            P("front", None, "blk"),
            P("front", "blk", None),
            P(),
            P("front", "blk", None),
            P(),
            P(),
        ),
        out_specs=(P("front", "blk", None), P("front", "blk", None), P(("front", "blk"), None)),
        check_vma=False,
    )
```

profile of v0, /device:TPU:1, one launch (start us, length us, event | category | flops | bytes accessed | tf_op | source)
XLA Modules:
  0.0 326.7 jit_solution(12871777678165630482)
XLA Ops:
  7.2 0.0 all-gather.5.cloned.1.call-start
  7.2 0.7 all-gather.5.cloned.1.call-update
  7.9 0.0 all-gather.9.cloned.1.call-start
  8.0 0.2 copy-done
  8.1 1.1 convolution_convert_fusion.2
  9.3 58.0 %all-gather.5.cloned.1.call-done = bf16[1,256,12288]{2,1,0:T(8,128)(2,1)} async-done(((bf16[1,256,384]{2,1,0:T(8,128)(2,1)}), bf16[1,256,12288]{2,1,0:T(8,128)(2,1)}) %all-gather.5.cloned.1.call-update) | async-done | bytes 6291472 | tf_op jit(solution)/shard_map/all_gather | solution.py:44
  67.3 10.9 %fusion = bf16[512,12288]{1,0:T(8,128)(2,1)} fusion(bf16[512,256]{1,0:T(8,128)(2,1)S(1)} %convolution_convert_fusion.2, bf16[1,512,12288]{2,1,0:T(8,128)(2,1)} %param.11, bf16[1,256,12288]{2,1,0:T(8,128)(2,1)} %all-gather.5.cloned.1.call-done), kind=kOutput, calls=%fused_computation.3 | convolution fusion | flops 3240099840 | bytes 31719424 | tf_op jit(solution)/shard_map/dot_general | solution.py:42
  78.2 9.8 %convolution_convert_fusion = bf16[512,256]{1,0:T(8,128)(2,1)S(1)} fusion(bf16[512,12288]{1,0:T(8,128)(2,1)} %fusion, bf16[12288,256]{1,0:T(8,128)(2,1)} %param.12), kind=kOutput, calls=%fused_computation.10 | convolution fusion | flops 3221356544 | bytes 19136512 | tf_op jit(solution)/shard_map/dot_general | solution.py:48
  88.0 0.9 convolution_convert_fusion.3
  88.9 0.0 all-gather.9.cloned.1.call-update
  88.9 0.0 reduce-scatter.2.cloned.1.call-start
  89.0 12.6 %fusion.32 = f32[12288,256]{1,0:T(8,128)} fusion(bf16[512,12288]{1,0:T(8,128)(2,1)} %fusion, bf16[512,256]{1,0:T(8,128)(2,1)S(1)} %convolution_convert_fusion), kind=kOutput, calls=%fused_computation.62 | convolution fusion | flops 3221225472 | bytes 25427968 | tf_op jit(solution)/shard_map/dot_general | solution.py:55
  101.5 0.0 reduce-scatter.2.cloned.1.call-update
  101.6 0.2 all-gather.7.cloned.1.call-start
  101.9 32.7 %all-gather.9.cloned.1.call-done = bf16[8192,256]{1,0:T(8,128)(2,1)} async-done(((bf16[256,256]{1,0:T(8,128)(2,1)}), bf16[8192,256]{1,0:T(8,128)(2,1)}) %all-gather.9.cloned.1.call-update) | async-done | bytes 4194320 | tf_op jit(solution)/shard_map/all_gather | solution.py:10
  134.6 2.8 convert_reduce_fusion
  137.4 0.1 copy.26
  137.6 11.7 %cholesky.50 = f32[128,128]{1,0:T(8,128)S(1)} custom-call(f32[128,128]{1,0:T(8,128)S(1)} %cholesky.118), custom_call_target="Cholesky" | custom-call | tf_op jit(solution)/shard_map/jit(cholesky)/cholesky | solution.py:20
  149.4 9.8 %custom-call.18 = f32[1,128,128]{1,2,0:T(8,128)S(1)} custom-call(f32[1,128,128]{2,1,0:T(8,128)S(1)} %get-tuple-element.36), custom_call_target="InvertDiagBlocksLowerTriangular" | custom-call | tf_op jit(solution)/shard_map/jit(cholesky)/cholesky | solution.py:20
  159.2 0.2 constant_dynamic-update-slice_fusion
  159.4 0.3 convolution_subtract_fusion.2
  159.7 11.7 %cholesky.105 = f32[128,128]{1,0:T(8,128)S(1)} custom-call(f32[128,128]{1,0:T(8,128)S(1)} %convolution_subtract_fusion.2), custom_call_target="Cholesky" | custom-call | tf_op jit(solution)/shard_map/jit(cholesky)/cholesky | solution.py:20
  171.4 0.7 compare_reduce_fusion
  173.4 0.1 triangular_solve.74
  173.5 4.1 %while.1 = (s32[]{:T(128)}, f32[256,256]{1,0:T(8,128)S(1)}, s32[2,2]{1,0:T(2,128)S(1)}, f32[2,128,128]{2,1,0:T(8,128)S(1)}, s32[]{:T(128)}) while((s32[]{:T(128)}, f32[256,256]{1,0:T(8,128)S(1)}, s32[2,2]{1,0:T(2,128)S(1)}, f32[2,128,128]{2,1,0:T(8,128)S(1)}, s32[]{:T(128)}) %tuple.32), condition=%wide.while_cond, body=%wide.while_body.sunk | while | flops 2 | bytes 131189 | solution.py:62
  173.7 0.6 fusion.48
  174.3 1.4 bitcast_dynamic-update-slice_fusion.2
  175.7 0.6 fusion.48
  176.3 1.4 bitcast_dynamic-update-slice_fusion.2
  177.6 19.7 %custom-call.19 = f32[2,128,128]{1,2,0:T(8,128)S(1)} custom-call(f32[2,128,128]{2,1,0:T(8,128)S(1)} %get-tuple-element.10), custom_call_target="InvertDiagBlocksLowerTriangular" | custom-call | tf_op jit(solution)/shard_map/jit(_solve_triangular)/triangular_solve | solution.py:62
  197.3 0.3 fusion.31
  197.6 0.6 convolution_subtract_fusion
  198.2 0.4 convolution_convert_fusion.4
  198.7 0.1 copy.37
  198.8 0.9 convolution_convert_fusion.1
  199.9 0.2 select_reduce_fusion
  200.1 39.9 %reduce-scatter.2.cloned.1.call-done = f32[384,256]{1,0:T(8,128)} async-done(((f32[12288,256]{1,0:T(8,128)}), f32[384,256]{1,0:T(8,128)}) %reduce-scatter.2.cloned.1.call-update) | async-done | bytes 393232 | tf_op jit(solution)/shard_map/reduce_scatter | solution.py:54
  240.0 1.4 fusion.15
  241.4 55.5 %all-gather.7.cloned.1.call-done = bf16[64,256,256]{2,1,0:T(8,128)(2,1)} async-done(((bf16[2,256,256]{2,1,0:T(8,128)(2,1)}), bf16[64,256,256]{2,1,0:T(8,128)(2,1)}) %all-gather.7.cloned.1.call-update) | async-done | bytes 8388624 | tf_op jit(solution)/shard_map/all_gather | solution.py:80
  296.9 8.0 %fusion.7 = bf16[256,4,256]{2,1,0:T(4,128)(2,1)S(1)} fusion(bf16[64,256,256]{2,1,0:T(8,128)(2,1)} %all-gather.7.cloned.1.call-done, s32[64]{0:T(128)S(1)} %dynamic-slice_bitcast_fusion, s32[4]{0:T(128)S(1)} %multiply_add_fusion), kind=kOutput, calls=%fused_computation.9 | convolution fusion | flops 33816832 | bytes 8913168 | tf_op jit(solution)/shard_map/gj,jxk->xgk/dot_general | solution.py:84
  304.9 0.9 copy.31
  305.8 4.1 %all-to-all-start = ((bf16[256,4,256]{2,0,1:T(8,128)(2,1)}), bf16[256,4,256]{2,0,1:T(8,128)(2,1)S(1)}, u32[]{:S(2)}, u32[]{:S(2)}) async-start(bf16[256,4,256]{2,0,1:T(8,128)(2,1)} %copy.31), calls=%async_computation.1 | async-start | bytes 1048576 | tf_op jit(solution)/shard_map/all_to_all | solution.py:87
  310.0 0.5 convolution_subtract_fusion.1
  310.4 0.4 fusion.23
  310.9 0.8 copy.33
  311.7 7.3 %all-to-all-done = bf16[256,4,256]{2,0,1:T(8,128)(2,1)S(1)} async-done(((bf16[256,4,256]{2,0,1:T(8,128)(2,1)}), bf16[256,4,256]{2,0,1:T(8,128)(2,1)S(1)}, u32[]{:S(2)}, u32[]{:S(2)}) %all-to-all-start) | async-done | bytes 524320 | tf_op jit(solution)/shard_map/all_to_all | solution.py:87
  319.0 0.2 copy.32
  319.2 1.0 copy.34
  (28 shorter events, 0.3 us)
Async XLA Ops:
  7.2 1.0 copy-start
  7.2 60.1 %all-gather.5.cloned.1.call-start = ((), (), s32[]{:S(2)}) async-start(), calls=%async_computation.2 | async-start | bytes 6488064 | tf_op jit(solution)/shard_map/all_gather | solution.py:44
  7.9 126.7 %all-gather.9.cloned.1.call-start = ((), (), s32[]{:S(2)}) async-start(), calls=%async_computation.5 | async-start | bytes 4325376 | tf_op jit(solution)/shard_map/all_gather | solution.py:10
  9.3 68.9 %copy-start.2 = (bf16[512,256]{1,0:T(8,128)(2,1)}, bf16[512,256]{1,0:T(8,128)(2,1)S(1)}, u32[]{:S(2)}) copy-start(bf16[512,256]{1,0:T(8,128)(2,1)S(1)} %convolution_convert_fusion.2) | copy-start | bytes 786436
  88.9 151.1 %reduce-scatter.2.cloned.1.call-start = ((), (), s32[]{:S(2)}) async-start(), calls=%async_computation.3 | async-start | bytes 12976128 | tf_op jit(solution)/shard_map/reduce_scatter | solution.py:54
  101.6 97.3 %copy-start.4 = (s32[1,2,256]{2,1,0:T(2,128)S(1)}, s32[1,2,256]{2,1,0:T(2,128)}, u32[]{:S(2)}) copy-start(s32[1,2,256]{2,1,0:T(2,128)} %param.13) | copy-start | bytes 6148
  101.6 98.3 %copy-start.5 = (s32[4,64]{1,0:T(4,128)S(1)}, s32[4,64]{1,0:T(4,128)}, u32[]{:S(2)}) copy-start(s32[4,64]{1,0:T(4,128)} %param.14) | copy-start | bytes 3076
  101.6 98.3 %copy-start.6 = (s32[96]{0:T(128)S(1)}, s32[96]{0:T(128)}, u32[]{:S(2)}) copy-start(s32[96]{0:T(128)} %param.15) | copy-start | bytes 1156
  101.6 195.3 %all-gather.7.cloned.1.call-start = ((), (), s32[]{:S(2)}) async-start(), calls=%async_computation.4 | async-start | bytes 8650752 | tf_op jit(solution)/shard_map/all_gather | solution.py:80
  240.0 69.9 %copy-start.3 = (f32[384,256]{1,0:T(8,128)S(1)}, f32[384,256]{1,0:T(8,128)}, u32[]{:S(2)}) copy-start(f32[384,256]{1,0:T(8,128)} %reduce-scatter.2.cloned.1.call-done) | copy-start | bytes 1179652
  240.0 80.2 %copy-start.1 = (bf16[1,512,256]{2,1,0:T(8,128)(2,1)S(1)}, bf16[1,512,256]{2,1,0:T(8,128)(2,1)}, u32[]{:S(2)}) copy-start(bf16[1,512,256]{2,1,0:T(8,128)(2,1)} %param.8) | copy-start | bytes 786436
  305.8 13.2 %all-to-all-start = ((bf16[256,4,256]{2,0,1:T(8,128)(2,1)}), bf16[256,4,256]{2,0,1:T(8,128)(2,1)S(1)}, u32[]{:S(2)}, u32[]{:S(2)}) async-start(bf16[256,4,256]{2,0,1:T(8,128)(2,1)} %copy.31), calls=%async_computation.1 | async-start | bytes 1048576 | tf_op jit(solution)/shard_map/all_to_all | solution.py:87
Sparse Core Ops, SparseCore 0:
  10.2 57.0 all-gather.4
  89.0 45.5 all-gather.8
  138.4 101.5 reduce-scatter.1
  242.7 54.1 all-gather.6
where the time goes:
time: 327 us
  waiting for transfers between devices  194 us (59%)
  other arithmetic  56.8 us (17%)
  matrix products  48.3 us (15%)
  between operations  15.3 us (5%)
  local copies, waits for them, and re-layouts  7.4 us (2%)
  starting transfers between devices  4.48 us (1%)
    all_gather x1, waiting for transfers between devices, body(): lax.all_gather(panel_rows, 'blk', axis=2, tiled=True)[0]  58 us
    all_gather x1, waiting for transfers between devices, body(): all_blocks = lax.all_gather(placed, 'blk', axis=0, tiled=True)  55.5 us
    reduce_scatter x1, waiting for transfers between devices, body(): lax.psum_scatter(lax.dot_general(window, sketched, (((0,), (0,)), ((), ()...  39.9 us
    another operation x6, other arithmetic, gram_factor(): return jnp.linalg.cholesky(gram_matrix)  34 us
    all_gather x1, waiting for transfers between devices, gathered_total(): return lax.all_gather(x, axis).astype(jnp.float32).sum(0)  32.7 us
    another operation x3, other arithmetic, body(): jax.scipy.linalg.solve_triangular(factor_low, cross_share.T, lower=True)  19.7 us
    dot_general x1, matrix products, body(): lax.dot_general(window, sketched, (((0,), (0,)), ((), ())), preferred_ele...  12.6 us
    dot_general x1, matrix products, body(): jnp.dot(factored, lax.all_gather(panel_rows, 'blk', axis=2, tiled=True)[0...  10.9 us
  transfers between devices with their start and end apart: 5, of which 5 were waited for; matrix products, arithmetic and copies ran while one was open for 25% of the time, Pallas kernels for 0%

commit v1 on v0

v1 whole, which is shorter than its diff:
```python
import math

import jax
import jax.numpy as jnp
from jax import lax
from jax.experimental import pallas as pl
from jax.experimental.pallas import tpu as pltpu
from jax.sharding import PartitionSpec as P

F32 = jnp.float32
BF16 = jnp.bfloat16
MESH = pl.DeviceIdType.MESH
VLIM = 62 * 1024 * 1024

ORDER = (
    (2, 2), (2, 0), (2, 1), (2, 3), (0, 2), (1, 2), (3, 2), (1, 1),
    (3, 3), (1, 3), (3, 1), (1, 0), (0, 1), (3, 0), (0, 3), (0, 0),
)


def dot(a, b):
    return jnp.dot(a, b, preferred_element_type=F32)


def split(a):
    high = a.astype(BF16)
    return high, (a - high.astype(F32)).astype(BF16)


def remote(src, dst, send_sem, recv_sem, where):
    return pltpu.make_async_remote_copy(
        src_ref=src,
        dst_ref=dst,
        send_sem=send_sem,
        recv_sem=recv_sem,
        device_id=where,
        device_id_type=MESH,
    )


def await_bytes(ref, sem):
    pltpu.make_async_copy(ref, ref, sem).wait()


def panel_kernel(
    col_ref, uinv_ref, prow_ref, t_hbm, om_hbm,
    l_out, s_out, gm_out, x_out,
    t_v, om_v, own_v, y_v, st_v,
    q_send, q_recv, q_bc, q_full, gm_send, gm_recv, gm_bc, gm_full,
    pair_s, pair_r, s1_s, s1_r, acc, s2_s, s2_r, s3_s, s3_r,
    ld_sem, ar_ss, ar_rs, pair_ss, pair_rs, s1_ss, s1_rs, s2_ss, s2_rs, s3_ss, s3_rs,
):
    me = lax.axis_index("blk")
    n = 32
    x, y, c = me // 8, (me // 2) % 4, me % 2
    cols = t_v.shape[1]
    wide = cols // n
    loads = 8
    step = cols // loads

    own_copy = pltpu.make_async_copy(
        om_hbm.at[pl.ds(pl.multiple_of(me * wide, wide), wide)], own_v, ld_sem.at[loads]
    )
    own_copy.start()
    copies = []
    for k in range(loads):
        part = pl.ds(k * step, step)
        pair = (
            pltpu.make_async_copy(om_hbm.at[part], om_v.at[part], ld_sem.at[loads + 1 + k]),
            pltpu.make_async_copy(t_hbm.at[:, part], t_v.at[:, part], ld_sem.at[k]),
        )
        for one in pair:
            one.start()
        copies.append(pair)

    barrier = pltpu.get_barrier_semaphore()

    @pl.loop(1, n)
    def _(i):
        pl.semaphore_signal(
            barrier, inc=1, device_id={"blk": lax.rem(me + i, n)}, device_id_type=MESH
        )

    def scatter(src, dst, phase):
        @pl.loop(1, n)
        def _(i):
            peer = lax.rem(me + i, n)
            remote(
                src.at[peer], dst.at[i], ar_ss.at[phase], ar_rs.at[phase], {"blk": peer}
            ).start()

    def spread(src, dst, phase):
        @pl.loop(1, n)
        def _(i):
            peer = lax.rem(me + i, n)
            remote(src, dst.at[me], ar_ss.at[phase], ar_rs.at[phase], {"blk": peer}).start()

    def all_came(dst, phase):
        await_bytes(dst.at[pl.ds(1, n - 1)], ar_rs.at[phase])

    own_copy.wait()
    q_send[...] = dot(prow_ref[...], own_v[...]).reshape(q_send.shape)
    factored = dot(col_ref[...], uinv_ref[...]).astype(BF16)
    l_out[...] = factored
    pl.semaphore_wait(barrier, n - 1)
    scatter(q_send, q_recv, 0)
    q_recv[0] = q_send[me]

    def sketch_step(k):
        for one in copies[k]:
            one.wait()
        part = pl.ds(k * step, step)
        out = dot(t_v[:, part], om_v[part, :])
        if k == 0:
            y_v[...] = out
        else:
            y_v[...] += out

    for k in range(loads // 2):
        sketch_step(k)
    all_came(q_recv, 0)
    total = jnp.sum(q_recv[...], axis=0)
    q_bc[...] = total
    q_full[me] = total
    spread(q_bc, q_full, 1)
    for k in range(loads // 2, loads):
        sketch_step(k)
    all_came(q_full, 1)
    q_high, q_low = split(q_full[...].reshape(256, 256))
    sk32 = y_v[...] - dot(factored, q_high) - dot(factored, q_low)
    sk = sk32.astype(BF16)
    s_out[...] = sk
    st_v[...] = sk32.T.astype(BF16)
    st = st_v[...]
    gram = dot(st, sk).reshape(n, 8, 256)
    mix = dot(st, factored).reshape(n, 8, 256)
    gm_send[...] = jnp.concatenate([gram, mix], axis=1).astype(BF16)
    scatter(gm_send, gm_recv, 2)
    gm_recv[0] = gm_send[me]

    def chip(dx, dy):
        return lax.rem(x + dx, 4) * 4 + lax.rem(y + dy, 4)

    def place(dx, dy):
        return {"blk": chip(dx, dy) * 2 + c}

    def chunk(owner):
        return dot(st_v[...], t_v[:, pl.ds(pl.multiple_of(owner * wide, 128), wide)])

    waits = []

    def send(src, dst, ss, rs, where):
        copy = remote(src, dst, ss, rs, where)
        copy.start()
        waits.append(copy)
        return copy

    partner = {"blk": chip(0, 0) * 2 + (1 - c)}
    pairs = []
    for i, (dx, dy) in enumerate(ORDER):
        pair_s[i] = chunk(chip(dx, dy) * 2 + (1 - c)).astype(BF16)
        pairs.append(send(pair_s.at[i], pair_r.at[i], pair_ss.at[i], pair_rs.at[i], partner))
        if i == 11:
            all_came(gm_recv, 2)
            total = jnp.sum(gm_recv[...].astype(F32), axis=0)
            gm_bc[...] = total
            gm_full[me] = total
            spread(gm_bc, gm_full, 3)

    first = {}
    towards = (
        (lambda d: place(d, 0), lambda d: place(0, d)),
        (lambda d: place(0, d), lambda d: place(d, 0)),
    )

    def handle(h, d1, d2, v):
        go = towards[h][0]
        if d1 == 0:
            acc[h, d2] = v
            return
        if d1 == 2:
            slot, where = d2, go(1) if d2 < 2 else go(3)
        else:
            if (d2 < 2) == (d1 == 1):
                first[h, d2].wait_recv()
                v = v + s1_r[h, d2].astype(F32)
            slot, where = (4 + d2, go(1)) if d1 == 1 else (8 + d2, go(3))
        s1_s[h, slot] = v.astype(BF16)
        first[h, slot] = send(
            s1_s.at[h, slot], s1_r.at[h, slot], s1_ss.at[h, slot], s1_rs.at[h, slot], where
        )

    for i, (dx, dy) in enumerate(ORDER):
        v = chunk(chip(dx, dy) * 2 + c)
        pairs[i].wait_recv()
        v = v + pair_r[i].astype(F32)
        handle(0, dx, dy, v[:128])
        handle(1, dy, dx, v[128:])

    half, full = {}, {}
    for d2 in (2, 1, 3, 0):
        for h in range(2):
            go = towards[h][1]
            first[h, 4 + d2].wait_recv()
            first[h, 8 + d2].wait_recv()
            v = acc[h, d2] + s1_r[h, 4 + d2].astype(F32) + s1_r[h, 8 + d2].astype(F32)
            if d2 == 2:
                for k in range(2):
                    s2_s[h, k] = v[64 * k : 64 * k + 64].astype(BF16)
                    half[h, k] = send(
                        s2_s.at[h, k], s2_r.at[h, k], s2_ss.at[h, k], s2_rs.at[h, k], go(1 + 2 * k)
                    )
            elif d2 == 0:
                for k in range(2):
                    full[h, k].wait_recv()
                    v = v + s3_r[h, k].astype(F32)
                x_out[h * 128 : h * 128 + 128, :] = v
            else:
                k = d2 // 2
                half[h, k].wait_recv()
                more = s2_r[h, k].astype(F32)
                low, high = v[:64], v[64:]
                if k == 0:
                    low = low + more
                else:
                    high = high + more
                s3_s[h, k, 0:64, :] = low.astype(BF16)
                s3_s[h, k, 64:128, :] = high.astype(BF16)
                full[h, k] = send(
                    s3_s.at[h, k], s3_r.at[h, k], s3_ss.at[h, k], s3_rs.at[h, k], go(d2)
                )
    all_came(gm_full, 3)
    gm_out[...] = gm_full[...]
    for copy in waits:
        copy.wait_send()
    await_bytes(q_send.at[pl.ds(1, n - 1)], ar_ss.at[0])
    await_bytes(q_full.at[pl.ds(1, n - 1)], ar_ss.at[1])
    await_bytes(gm_send.at[pl.ds(1, n - 1)], ar_ss.at[2])
    await_bytes(gm_full.at[pl.ds(1, n - 1)], ar_ss.at[3])


def panel_call(column, inverse, rows, trailing, sketch):
    length, cols = trailing.shape
    wide = rows.shape[1]
    vmem = pl.BlockSpec(memory_space=pltpu.VMEM)
    anyw = pl.BlockSpec(memory_space=pl.ANY)
    dma = pltpu.SemaphoreType.DMA
    return pl.pallas_call(
        panel_kernel,
        out_shape=(
            jax.ShapeDtypeStruct((length, 256), BF16),
            jax.ShapeDtypeStruct((length, 256), BF16),
            jax.ShapeDtypeStruct((32, 16, 256), F32),
            jax.ShapeDtypeStruct((256, wide), F32),
        ),
        in_specs=[vmem, vmem, vmem, anyw, anyw],
        out_specs=(vmem, vmem, vmem, vmem),
        scratch_shapes=[
            pltpu.VMEM((length, cols), BF16),
            pltpu.VMEM((cols, 256), BF16),
            pltpu.VMEM((wide, 256), BF16),
            pltpu.VMEM((length, 256), F32),
            pltpu.VMEM((256, length), BF16),
            pltpu.VMEM((32, 8, 256), F32),
            pltpu.VMEM((32, 8, 256), F32),
            pltpu.VMEM((8, 256), F32),
            pltpu.VMEM((32, 8, 256), F32),
            pltpu.VMEM((32, 16, 256), BF16),
            pltpu.VMEM((32, 16, 256), BF16),
            pltpu.VMEM((16, 256), F32),
            pltpu.VMEM((32, 16, 256), F32),
            pltpu.VMEM((16, 256, wide), BF16),
            pltpu.VMEM((16, 256, wide), BF16),
            pltpu.VMEM((2, 12, 128, wide), BF16),
            pltpu.VMEM((2, 12, 128, wide), BF16),
            pltpu.VMEM((2, 4, 128, wide), F32),
            pltpu.VMEM((2, 2, 64, wide), BF16),
            pltpu.VMEM((2, 2, 64, wide), BF16),
            pltpu.VMEM((2, 2, 128, wide), BF16),
            pltpu.VMEM((2, 2, 128, wide), BF16),
            dma((17,)),
            dma((4,)),
            dma((4,)),
            dma((16,)),
            dma((16,)),
            dma((2, 12)),
            dma((2, 12)),
            dma((2, 2)),
            dma((2, 2)),
            dma((2, 2)),
            dma((2, 2)),
        ],
        compiler_params=pltpu.CompilerParams(
            collective_id=0, has_side_effects=True, vmem_limit_bytes=VLIM
        ),
        name="panel",
    )(column, inverse, rows, trailing, sketch)


def inverse_factor(a_ref, block=64):
    size = a_ref.shape[0]
    lane = lax.broadcasted_iota(jnp.int32, (8, size), 1)
    sub = lax.broadcasted_iota(jnp.int32, (8, 1), 0)
    for k in range(size // block):
        base = k * block
        tiles = [a_ref[base + 8 * t : base + 8 * t + 8, :] for t in range(block // 8)]
        pivots = [jnp.ones((8, 1), F32) for _ in tiles]
        for j in range(block):
            at, row = base + j, j % 8
            here = lane == at
            mine = tiles[j // 8]
            pivot_row = mine[row : row + 1, :]
            pivot = pivot_row[:, at : at + 1]
            scaled = jnp.where(here[:1], 1.0, pivot_row) * (1.0 / pivot)
            pivots[j // 8] = jnp.where(sub == row, pivot, pivots[j // 8])
            for t in range(j // 8, block // 8):
                tile = tiles[t]
                factor = tile[:, at : at + 1]
                if t == j // 8:
                    below = sub > row
                    factor = jnp.where(below, factor, 0.0)
                    kept = jnp.where(here, jnp.where(sub == row, 1.0, jnp.where(below, 0.0, tile)), tile)
                else:
                    kept = jnp.where(here, 0.0, tile)
                tiles[t] = kept - factor * scaled
        rest = base + block
        for t in range(block // 8):
            stale = (lane > sub + (base + 8 * t)) & (lane < rest)
            tile = jnp.where(stale, 0.0, tiles[t] * lax.rsqrt(pivots[t]))
            a_ref[base + 8 * t : base + 8 * t + 8, :] = tile
        if rest < size:
            done = a_ref[base:rest, :]
            change = lax.dot_general(
                done[:, rest:],
                done,
                (((0,), (0,)), ((), ())),
                precision=lax.Precision.HIGHEST,
                preferred_element_type=F32,
            )
            column = lax.broadcasted_iota(jnp.int32, (size - rest, size), 1)
            inside = (column >= base) & (column < rest)
            a_ref[rest:, :] = jnp.where(inside, 0.0, a_ref[rest:, :]) - change


def factor_kernel(slab_rows, s_ref, gm_ref, x_ref, prow_ref, map_ref, right_ref, left_ref, a_ref):
    size = 256
    a_ref[...] = gm_ref[:, :8, :].reshape(size, size) * (1.0 / slab_rows)
    inverse_factor(a_ref)
    row = lax.broadcasted_iota(jnp.int32, (size, size), 0)
    column = lax.broadcasted_iota(jnp.int32, (size, size), 1)
    w = jnp.where(column <= row, a_ref[...], 0.0)
    mix_high, mix_low = split(gm_ref[:, 8:, :].reshape(size, size))
    cross = x_ref[...] - dot(mix_high, prow_ref[...]) - dot(mix_low, prow_ref[...])
    w_high, w_low = split(w)
    c_high, c_low = split(cross)
    right = dot(w_high, c_high) + dot(w_high, c_low) + dot(w_low, c_high)
    right_ref[...] = (right.T * (1.0 / math.sqrt(slab_rows))).astype(BF16)
    turn = (((1,), (1,)), ((), ()))
    sk = s_ref[...]
    left = lax.dot_general(sk, w_high, turn, preferred_element_type=F32)
    left = (left + lax.dot_general(sk, w_low, turn, preferred_element_type=F32)).astype(BF16)
    for k in range(2):
        pick = (map_ref[k : k + 1, :] == row).astype(BF16)
        left_ref[k] = dot(pick, left[k * size : k * size + size]).astype(BF16)


def factor_call(slab_rows, sk, gm, xt, rows, row_map):
    wide = rows.shape[1]
    vmem = pl.BlockSpec(memory_space=pltpu.VMEM)

    def body(*refs):
        factor_kernel(slab_rows, *refs)

    return pl.pallas_call(
        body,
        out_shape=(
            jax.ShapeDtypeStruct((wide, 256), BF16),
            jax.ShapeDtypeStruct((2, 256, 256), BF16),
        ),
        in_specs=[vmem] * 5,
        out_specs=(vmem, vmem),
        scratch_shapes=[pltpu.VMEM((256, 256), F32)],
        compiler_params=pltpu.CompilerParams(vmem_limit_bytes=32 * 1024 * 1024),
        name="factor",
    )(sk, gm, xt, rows, row_map)


def place_kernel(table, in_ref, out_ref, buf_a, stage, buf_b, buf_c, a_ss, a_rs, b_ss, b_rs, c_ss, c_rs):
    me = lax.axis_index("blk")
    front = lax.axis_index("front")
    n, fronts = 32, 4
    barrier = pltpu.get_barrier_semaphore()

    @pl.loop(1, n)
    def _(i):
        pl.semaphore_signal(
            barrier, inc=1, device_id={"blk": lax.rem(me + i, n)}, device_id_type=MESH
        )

    for i in range(1, fronts):
        pl.semaphore_signal(
            barrier, inc=1, device_id={"front": lax.rem(front + i, fronts)}, device_id_type=MESH
        )
    pl.semaphore_wait(barrier, n - 1 + fronts - 1)

    @pl.loop(1, n)
    def _(i):
        peer = lax.rem(me + i, n)
        remote(in_ref.at[peer], buf_a.at[me], a_ss, a_rs, {"blk": peer}).start()

    buf_a[me] = in_ref[me]
    buf_a[n] = jnp.zeros(buf_a.shape[1:], BF16)
    await_bytes(buf_a.at[pl.ds(0, n - 1)], a_rs)

    def choose(g):
        @pl.loop(0, n)
        def _(t):
            j = table[g * n + t]
            stage[g, t] = buf_a[j // 2, lax.rem(j, 2)]

    sends = []
    for i in range(1, fronts):
        g = lax.rem(front + i, fronts)
        choose(g)
        copy = remote(stage.at[g], buf_b.at[front], b_ss.at[i], b_rs.at[i], {"front": g})
        copy.start()
        sends.append(copy)
    choose(front)
    buf_b[front] = stage[front]
    for copy in sends:
        copy.wait_recv()

    @pl.loop(1, n)
    def _(i):
        peer = lax.rem(me + i, n)
        remote(buf_b.at[:, peer], buf_c.at[me], c_ss, c_rs, {"blk": peer}).start()

    buf_c[me] = buf_b[:, me]
    await_bytes(buf_c.at[pl.ds(0, n - 1)], c_rs)
    out_ref[...] = buf_c[...]
    for copy in sends:
        copy.wait_send()
    await_bytes(in_ref.at[pl.ds(0, n - 1)], a_ss)
    await_bytes(buf_c.at[pl.ds(0, n - 1)], c_ss)


def place_call(table, pieces):
    vmem = pl.BlockSpec(memory_space=pltpu.VMEM)
    dma = pltpu.SemaphoreType.DMA
    return pl.pallas_call(
        place_kernel,
        out_shape=jax.ShapeDtypeStruct((32, 4, 16, 128), BF16),
        in_specs=[pl.BlockSpec(memory_space=pltpu.SMEM), vmem],
        out_specs=vmem,
        scratch_shapes=[
            pltpu.VMEM((33, 2, 16, 128), BF16),
            pltpu.VMEM((4, 32, 16, 128), BF16),
            pltpu.VMEM((4, 32, 16, 128), BF16),
            pltpu.VMEM((32, 4, 16, 128), BF16),
            dma(()),
            dma(()),
            dma((4,)),
            dma((4,)),
            dma(()),
            dma(()),
        ],
        compiler_params=pltpu.CompilerParams(
            collective_id=1, has_side_effects=True, vmem_limit_bytes=32 * 1024 * 1024
        ),
        name="place",
    )(table, pieces)


def body(
    panel_column, upper_inverse, panel_rows, trailing, sketch, row_map, parent_block, parent_slot
):
    slab_rows = trailing.shape[1] * lax.axis_size("blk")
    front = lax.axis_index("front")
    factored, sk, gm, xt = panel_call(
        panel_column[0], upper_inverse[0], panel_rows[0], trailing[0], sketch
    )
    blocks = lax.dynamic_slice(parent_block, (front, 0), (1, parent_block.shape[1]))[0]
    parents = jnp.arange(parent_slot.shape[0], dtype=jnp.int32)
    owners = jnp.sum(jnp.where(blocks[:, None] == parents[None, :], parent_slot[None, :], 0), axis=1)
    device = jnp.arange(128, dtype=jnp.int32)
    number = jnp.arange(blocks.shape[0], dtype=jnp.int32)
    table = 64 + jnp.sum(
        jnp.where(owners[None, :] == device[:, None], number[None, :] - 64, 0), axis=1
    )
    right, left = factor_call(slab_rows, sk, gm, xt, panel_rows[0], row_map[0])
    pieces = left.reshape(2, 32, 8, 2, 128).transpose(1, 0, 3, 2, 4).reshape(32, 2, 16, 128)
    placed = place_call(table, pieces)
    parent = placed.reshape(32, 4, 2, 8, 128).transpose(0, 3, 1, 2, 4).reshape(256, 1024)
    return factored[None], right[None], parent


def solution(mesh):
    return jax.shard_map(
        body,
        mesh=mesh,
        in_specs=(
            P("front", "blk", None),
            P("front", None, None),
            P("front", None, "blk"),
            P("front", "blk", None),
            P(),
            P("front", "blk", None),
            P(),
            P(),
        ),
        out_specs=(P("front", "blk", None), P("front", "blk", None), P(("front", "blk"), None)),
        check_vma=False,
    )
```

time: 327 us -> 122 us (0.37)
  waiting for transfers between devices: 194 us -> 0 us
  Pallas kernels: 0 us -> 115 us
  other arithmetic: 56.8 us -> 0.29 us
  matrix products: 48.3 us -> 0 us
  between operations: 15.3 us -> 0.73 us
  starting transfers between devices: 4.48 us -> 0 us
    all_gather x3 -> x0, waiting for transfers between devices: 146 us -> none  [the longest x1 58 us: body(): lax.all_gather(panel_rows, 'blk', axis=2, tiled=True)[0]]
    pallas_call x0 -> x3, Pallas kernels: none -> 115 us  [the longest x1 59 us: panel_call(): pl.pallas_call(panel_kernel, out_shape=(jax.ShapeDtypeStruct((length, 256...]
    another operation x9 -> x0, other arithmetic: 53.7 us -> none  [the longest x6 34 us: gram_factor(): return jnp.linalg.cholesky(gram_matrix)]
    dot_general x7 -> x0, matrix products: 44.3 us -> none  [the longest x1 12.6 us: body(): lax.dot_general(window, sketched, (((0,), (0,)), ((), ())), preferred_ele...]
    reduce_scatter x1 -> x0, waiting for transfers between devices: 39.9 us -> none  [body(): lax.psum_scatter(lax.dot_general(window, sketched, (((0,), (0,)), ((), ()...]
    all_to_all x1 -> x0, waiting for transfers between devices: 7.27 us -> none  [body(): lax.all_to_all(outgoing, 'front', split_axis=1, concat_axis=1, tiled=True)]
    all_to_all x1 -> x0, starting transfers between devices: 4.14 us -> none  [body(): lax.all_to_all(outgoing, 'front', split_axis=1, concat_axis=1, tiled=True)]
    another operation x8 -> x0, matrix products: 4.07 us -> none  [the longest x3 2.28 us: body(): jax.scipy.linalg.solve_triangular(factor_low, cross_share.T, lower=True)]
  transfers between devices with their start and end apart: 5 -> 0, of which waited for: 5 -> 0; matrix products, arithmetic and copies ran while one was open for 25% -> 0% of each run, Pallas kernels for 0% -> 0%
where the time goes in v1:
time: 122 us
  Pallas kernels  115 us (94%)
  local copies, waits for them, and re-layouts  5.49 us (4%)
    pallas_call x1, Pallas kernels, panel_call(): pl.pallas_call(panel_kernel, out_shape=(jax.ShapeDtypeStruct((length, 256...  59 us
    pallas_call x1, Pallas kernels, place_call(): pl.pallas_call(place_kernel, out_shape=jax.ShapeDtypeStruct((32, 4, 16, 1...  32.4 us
    pallas_call x1, Pallas kernels, factor_call(): pl.pallas_call(body, out_shape=(jax.ShapeDtypeStruct((wide, 256), BF16),...  23.9 us
    unnamed x16, local copies, waits for them, and re-layouts  5.46 us

profile of v1, /device:TPU:1, one launch (start us, length us, event | category | flops | bytes accessed | tf_op | source)
XLA Modules:
  0.0 121.8 jit_solution(12802384083458060745)
XLA Ops:
  0.6 0.0 copy-start
  0.6 0.0 copy-start.1
  0.7 0.0 copy-start.5
  0.7 0.0 copy-start.6
  0.7 59.0 %panel.1 = (bf16[512,256]{1,0:T(8,128)(2,1)}, bf16[512,256]{1,0:T(8,128)(2,1)}, f32[32,16,256]{2,1,0:T(8,128)}, f32[256,384]{1,0:T(8,128)}) custom-call(bf16[512,256]{1,0:T(8,128)(2,1)} %bitcast.26, bf16[256,256]{1,0:T(8,128)(2,1)} %bitcast.28, bf16[256,384]{1,0:T(8,128)(2,1)} %bitcast.22, bf16[512,12288]{1,0:T(8,128)(2,1)} %bitcast.25, ...), custom_call_target="tpu_custom_call" | custom-call | tf_op jit(solution)/shard_map/panel/pallas_call | solution.py:248
  59.6 0.0 copy-done.1
  59.7 0.0 copy-done.5
  59.7 0.0 copy-start.2
  59.7 1.0 copy-done.2
  60.7 0.0 copy-start.3
  60.7 1.0 copy-done.3
  61.7 0.0 copy-start.4
  61.7 0.9 copy-done.4
  62.7 23.9 %factor.1 = (bf16[384,256]{1,0:T(8,128)(2,1)}, bf16[2,256,256]{2,1,0:T(8,128)(2,1)S(1)}) custom-call(bf16[512,256]{1,0:T(8,128)(2,1)S(1)} %copy-done.4, f32[32,16,256]{2,1,0:T(8,128)S(1)} %copy-done.2, f32[256,384]{1,0:T(8,128)S(1)} %copy-done.3, bf16[256,384]{1,0:T(8,128)(2,1)S(1)} %bitcast.23, s32[2,256]{1,0:T(2,128)S(1)} %bitcast.24), custom_call_target="tpu_custom_call" | custom-call | tf_op jit(solution)/shard_map/factor/pallas_call | solution.py:374
  86.6 0.0 copy-done
  86.6 0.0 copy-done.6
  86.6 0.2 select_reduce_fusion.1
  86.8 0.1 select_reduce_fusion
  86.9 32.4 %place.1 = bf16[32,4,16,128]{3,2,1,0:T(8,128)(2,1)S(1)} custom-call(s32[128]{0:T(128)S(1)} %broadcast_add_fusion.table, bf16[32,2,16,128]{3,2,1,0:T(8,128)(2,1)S(1)} %copy_bitcast_fusion.in_ref), custom_call_target="tpu_custom_call" | custom-call | tf_op jit(solution)/shard_map/place/pallas_call | solution.py:450
  119.3 1.7 %copy.16 = bf16[1,512,256]{2,1,0:T(8,128)(2,1)} copy(bf16[1,512,256]{2,1,0:T(8,128)(2,1)} %bitcast.27) | data formatting | bytes 524288
  121.0 0.8 copy.17
  (4 shorter events, 0.0 us)
Async XLA Ops:
  0.6 86.0 %copy-start = (s32[4,64]{1,0:T(4,128)S(1)}, s32[4,64]{1,0:T(4,128)}, u32[]{:S(2)}) copy-start(s32[4,64]{1,0:T(4,128)} %param.14) | copy-start | bytes 3076
  0.6 59.0 %copy-start.1 = (bf16[1,256,384]{2,1,0:T(8,128)(2,1)S(1)}, bf16[1,256,384]{2,1,0:T(8,128)(2,1)}, u32[]{:S(2)}) copy-start(bf16[1,256,384]{2,1,0:T(8,128)(2,1)} %param.10) | copy-start | bytes 589828
  0.7 59.0 %copy-start.5 = (s32[1,2,256]{2,1,0:T(2,128)S(1)}, s32[1,2,256]{2,1,0:T(2,128)}, u32[]{:S(2)}) copy-start(s32[1,2,256]{2,1,0:T(2,128)} %param.13) | copy-start | bytes 6148
  0.7 85.9 %copy-start.6 = (s32[96]{0:T(128)S(1)}, s32[96]{0:T(128)}, u32[]{:S(2)}) copy-start(s32[96]{0:T(128)} %param.15) | copy-start | bytes 1156
  59.7 1.0 copy-start.2
  60.7 1.0 copy-start.3
  61.7 0.9 copy-start.4

commit v2 on v0

v2 whole, which is shorter than its diff:
```python
import math

import jax
import jax.numpy as jnp
from jax import lax
from jax.experimental import pallas as pl
from jax.experimental.pallas import tpu as pltpu
from jax.sharding import PartitionSpec as P

F32 = jnp.float32
BF16 = jnp.bfloat16
MESH = pl.DeviceIdType.MESH
VLIM = 62 * 1024 * 1024

ORDER = (
    (2, 2), (2, 0), (2, 1), (2, 3), (0, 2), (1, 2), (3, 2), (1, 1),
    (3, 3), (1, 3), (3, 1), (1, 0), (0, 1), (3, 0), (0, 3), (0, 0),
)


def dot(a, b):
    return jnp.dot(a, b, preferred_element_type=F32)


def split(a):
    high = a.astype(BF16)
    return high, (a - high.astype(F32)).astype(BF16)


def remote(src, dst, send_sem, recv_sem, where):
    return pltpu.make_async_remote_copy(
        src_ref=src,
        dst_ref=dst,
        send_sem=send_sem,
        recv_sem=recv_sem,
        device_id=where,
        device_id_type=MESH,
    )


def await_bytes(ref, sem):
    pltpu.make_async_copy(ref, ref, sem).wait()


def factor_steps(a_ref, block=64, width=8, every=16):
    size = a_ref.shape[0]
    shape = (8, size)
    lane = lax.broadcasted_iota(jnp.int32, shape, 1)
    sub = lax.broadcasted_iota(jnp.int32, shape, 0)
    for k in range(size // block):
        base = k * block
        rest = base + block
        tiles = [a_ref[base + 8 * t : base + 8 * t + 8, :] for t in range(block // 8)]
        pivots = [jnp.ones(shape, F32) for _ in tiles]
        for j in range(0, block, width):
            at, low, own = base + j, j % 8, j // 8
            inside = (lane >= at) & (lane < at + width)

            def columns(tile):
                return [jnp.broadcast_to(tile[:, at + i : at + i + 1], shape) for i in range(width)]

            def line(tile, i):
                return jnp.broadcast_to(tile[low + i : low + i + 1, :], shape)

            mine = tiles[own]
            heads = columns(mine)
            m = [
                [line(heads[q], i) if q >= i else None for q in range(width)]
                for i in range(width)
            ]
            lines = [
                jnp.where(inside, jnp.where(lane == at + i, 1.0, 0.0), line(mine, i))
                for i in range(width)
            ]
            scales, mults = [], {}
            for i in range(width):
                inv = 1.0 / m[i][i]
                scales.append(inv)
                for q in range(i + 1, width):
                    mults[q, i] = m[i][q] * inv
                for q in range(i + 1, width):
                    for p in range(q, width):
                        m[q][p] = m[q][p] - mults[q, i] * m[i][p]
            for i in range(width):
                for q in range(i + 1, width):
                    lines[q] = lines[q] - mults[q, i] * lines[i]
            scaled = [lines[i] * scales[i] for i in range(width)]
            for t in range(own, block // 8):
                tile = tiles[t]
                cs = heads if t == own else columns(tile)
                cs = list(cs)
                for i in range(width):
                    for q in range(i + 1, width):
                        cs[q] = cs[q] - mults[q, i] * cs[i]
                out = jnp.where(inside, 0.0, tile)
                for i in range(width):
                    out = out - cs[i] * scaled[i]
                if t == own:
                    out = jnp.where(sub >= low + width, out, tile)
                    for i in range(width):
                        out = jnp.where(sub == low + i, lines[i], out)
                        pivots[t] = jnp.where(sub == low + i, m[i][i], pivots[t])
                tiles[t] = out
            if (j + width) % every == 0 and j + width < block:
                yield at + width
        for t in range(block // 8):
            stale = (lane > sub + (base + 8 * t)) & (lane < rest)
            tile = jnp.where(stale, 0.0, tiles[t] * lax.rsqrt(pivots[t]))
            a_ref[base + 8 * t : base + 8 * t + 8, :] = tile
        if rest < size:
            done = a_ref[base:rest, :]
            change = lax.dot_general(
                done[:, rest:],
                done,
                (((0,), (0,)), ((), ())),
                precision=lax.Precision.HIGHEST,
                preferred_element_type=F32,
            )
            column = lax.broadcasted_iota(jnp.int32, (size - rest, size), 1)
            within = (column >= base) & (column < rest)
            a_ref[rest:, :] = jnp.where(within, 0.0, a_ref[rest:, :]) - change
        yield rest


def fused_kernel(
    slab_rows,
    table, col_ref, uinv_ref, prow_ref, map_ref, t_hbm, om_hbm,
    l_out, right_out, z_out,
    t_v, om_v, own_v, y_v, st_v,
    q_send, q_recv, q_bc, q_full, gm_send, gm_recv, g_bc, g_full, m_bc, m_full,
    pair_s, pair_r, s1_s, s1_r, acc, s2_s, s2_r, s3_s, s3_r, x_v, a_ref,
    a0, a3, c1, c4, big, z_s, z_r,
    ld_sem, ar_ss, ar_rs, pair_ss, pair_rs, s1_ss, s1_rs, s2_ss, s2_rs, s3_ss, s3_rs,
    z_ss, z_rs,
):
    me = lax.axis_index("blk")
    front = lax.axis_index("front")
    n, fronts, size = 32, 4, 256
    x, y, c = me // 8, (me // 2) % 4, me % 2
    cols = t_v.shape[1]
    wide = cols // n
    loads = 8
    step = cols // loads

    barrier = pltpu.get_barrier_semaphore()

    @pl.loop(1, n)
    def _(i):
        pl.semaphore_signal(
            barrier, inc=1, device_id={"blk": lax.rem(me + i, n)}, device_id_type=MESH
        )

    for i in range(1, fronts):
        pl.semaphore_signal(
            barrier, inc=1, device_id={"front": lax.rem(front + i, fronts)}, device_id_type=MESH
        )

    own_copy = pltpu.make_async_copy(
        om_hbm.at[pl.ds(pl.multiple_of(me * wide, wide), wide)], own_v, ld_sem.at[loads]
    )
    own_copy.start()
    copies = []
    for k in range(loads):
        part = pl.ds(k * step, step)
        pair = (
            pltpu.make_async_copy(om_hbm.at[part], om_v.at[part], ld_sem.at[loads + 1 + k]),
            pltpu.make_async_copy(t_hbm.at[:, part], t_v.at[:, part], ld_sem.at[k]),
        )
        for one in pair:
            one.start()
        copies.append(pair)

    def scatter(src, dst, phase):
        @pl.loop(1, n)
        def _(i):
            peer = lax.rem(me + i, n)
            remote(
                src.at[peer], dst.at[i], ar_ss.at[phase], ar_rs.at[phase], {"blk": peer}
            ).start()

    def spread(src, dst, phase):
        @pl.loop(1, n)
        def _(i):
            peer = lax.rem(me + i, n)
            remote(src, dst.at[me], ar_ss.at[phase], ar_rs.at[phase], {"blk": peer}).start()

    def all_came(dst, phase):
        await_bytes(dst.at[pl.ds(1, n - 1)], ar_rs.at[phase])

    def chip(dx, dy):
        return lax.rem(x + dx, 4) * 4 + lax.rem(y + dy, 4)

    def place(dx, dy):
        return {"blk": chip(dx, dy) * 2 + c}

    partner = {"blk": chip(0, 0) * 2 + (1 - c)}
    waits = []

    def send(src, dst, ss, rs, where):
        copy = remote(src, dst, ss, rs, where)
        copy.start()
        waits.append(copy)
        return copy

    own_copy.wait()
    q_send[...] = dot(prow_ref[...], own_v[...]).reshape(q_send.shape)
    factored = dot(col_ref[...], uinv_ref[...]).astype(BF16)
    l_out[...] = factored
    pl.semaphore_wait(barrier, n - 1 + fronts - 1)
    scatter(q_send, q_recv, 0)
    q_recv[0] = q_send[me]

    def sketch_step(k):
        for one in copies[k]:
            one.wait()
        part = pl.ds(k * step, step)
        out = dot(t_v[:, part], om_v[part, :])
        if k == 0:
            y_v[...] = out
        else:
            y_v[...] += out

    for k in range(loads // 2):
        sketch_step(k)
    all_came(q_recv, 0)
    total = jnp.sum(q_recv[...], axis=0)
    q_bc[...] = total
    q_full[me] = total
    spread(q_bc, q_full, 1)
    for k in range(loads // 2, loads):
        sketch_step(k)
    all_came(q_full, 1)
    q_high, q_low = split(q_full[...].reshape(size, size))
    sk32 = y_v[...] - dot(factored, q_high) - dot(factored, q_low)
    sk = sk32.astype(BF16)
    st_v[...] = sk32.T.astype(BF16)
    st = st_v[...]
    gram = dot(st, sk).reshape(n, 8, size)
    mix = dot(st, factored).reshape(n, 8, size)
    gm_send[...] = jnp.concatenate([gram, mix], axis=1).astype(BF16)
    scatter(gm_send, gm_recv, 2)
    gm_recv[0] = gm_send[me]
    row = lax.broadcasted_iota(jnp.int32, (size, size), 0)
    for k in range(2):
        pick = (map_ref[k : k + 1, :] == row).astype(BF16)
        moved = dot(pick, sk[k * size : k * size + size]).astype(BF16)
        for h in range(2):
            a0[:, h, k] = moved[:, 128 * h : 128 * h + 128].reshape(16, 16, 128)

    @pl.loop(1, n)
    def _(i):
        peer = lax.rem(me + i, n)
        remote(
            a0.at[peer // 2, lax.rem(peer, 2)],
            a3.at[pl.ds(2 * me, 2)],
            ar_ss.at[5],
            ar_rs.at[5],
            {"blk": peer},
        ).start()

    a3[pl.ds(2 * me, 2)] = a0[me // 2, c]
    a3[2 * n] = jnp.zeros((16, 128), BF16)

    def choose():
        await_bytes(a3.at[pl.ds(0, 2 * n - 2)], ar_rs.at[5])

        @pl.loop(0, n)
        def _(t):
            for g in range(fronts):
                c1[t, g] = a3[table[t * fronts + g]]

        @pl.loop(1, n)
        def _(i):
            peer = lax.rem(me + i, n)
            remote(
                c1.at[peer], c4.at[me // 2, c], ar_ss.at[6], ar_rs.at[6], {"blk": peer}
            ).start()

        c4[me // 2, c] = c1[me]

    def assemble():
        await_bytes(c1.at[pl.ds(0, n - 1)], ar_rs.at[6])
        for g in range(fronts):
            for h in range(2):
                big[g * size : g * size + size, 128 * h : 128 * h + 128] = c4[:, h, g].reshape(
                    size, 128
                )

    def chunk(owner):
        return dot(st_v[...], t_v[:, pl.ds(pl.multiple_of(owner * wide, 128), wide)])

    first, half, full = {}, {}, {}
    towards = (
        (lambda d: place(d, 0), lambda d: place(0, d)),
        (lambda d: place(0, d), lambda d: place(d, 0)),
    )

    def handle(h, d1, d2, v):
        go = towards[h][0]
        if d1 == 0:
            acc[h, d2] = v
            return
        if d1 == 2:
            slot, where = d2, go(1) if d2 < 2 else go(3)
        else:
            if (d2 < 2) == (d1 == 1):
                first[h, d2].wait_recv()
                v = v + s1_r[h, d2].astype(F32)
            slot, where = (4 + d2, go(1)) if d1 == 1 else (8 + d2, go(3))
        s1_s[h, slot] = v.astype(BF16)
        first[h, slot] = send(
            s1_s.at[h, slot], s1_r.at[h, slot], s1_ss.at[h, slot], s1_rs.at[h, slot], where
        )

    pairs = []

    def theirs(i):
        dx, dy = ORDER[i]
        pair_s[i] = chunk(chip(dx, dy) * 2 + (1 - c)).astype(BF16)
        pairs.append(send(pair_s.at[i], pair_r.at[i], pair_ss.at[i], pair_rs.at[i], partner))

    def ours(i):
        dx, dy = ORDER[i]
        v = chunk(chip(dx, dy) * 2 + c)
        pairs[i].wait_recv()
        v = v + pair_r[i].astype(F32)
        handle(0, dx, dy, v[:128])
        handle(1, dy, dx, v[128:])

    def second(d2, h):
        go = towards[h][1]
        first[h, 4 + d2].wait_recv()
        first[h, 8 + d2].wait_recv()
        v = acc[h, d2] + s1_r[h, 4 + d2].astype(F32) + s1_r[h, 8 + d2].astype(F32)
        if d2 == 2:
            for k in range(2):
                s2_s[h, k] = v[64 * k : 64 * k + 64].astype(BF16)
                half[h, k] = send(
                    s2_s.at[h, k], s2_r.at[h, k], s2_ss.at[h, k], s2_rs.at[h, k], go(1 + 2 * k)
                )
        elif d2 == 0:
            for k in range(2):
                full[h, k].wait_recv()
                v = v + s3_r[h, k].astype(F32)
            x_v[h * 128 : h * 128 + 128, :] = v
        else:
            k = d2 // 2
            half[h, k].wait_recv()
            more = s2_r[h, k].astype(F32)
            low, high = v[:64], v[64:]
            if k == 0:
                low = low + more
            else:
                high = high + more
            s3_s[h, k, 0:64, :] = low.astype(BF16)
            s3_s[h, k, 64:128, :] = high.astype(BF16)
            full[h, k] = send(s3_s.at[h, k], s3_r.at[h, k], s3_ss.at[h, k], s3_rs.at[h, k], go(d2))

    turn = (((1,), (1,)), ((), ()))
    z_sends = []

    def leave(h):
        low, up = 128 * h, 128 * h + 128
        lane = lax.broadcasted_iota(jnp.int32, (128, size), 1)
        line = lax.broadcasted_iota(jnp.int32, (128, size), 0) + low
        w_high, w_low = split(jnp.where(lane <= line, a_ref[low:up, :], 0.0))
        left = lax.dot_general(big[...], w_high, turn, preferred_element_type=F32)
        left = left + lax.dot_general(big[...], w_low, turn, preferred_element_type=F32)
        z_s[h] = left.astype(BF16).reshape(fronts, size, 128)
        for i in (2, 1, 3):
            g = lax.rem(front + i, fronts)
            z_sends.append(
                send(z_s.at[h, g], z_r.at[h, front], z_ss.at[h, i], z_rs.at[h, i], {"front": g})
            )
        z_r[h, front] = z_s[h, front]

    for i in range(16):
        theirs(i)
        if i >= 12:
            ours(i - 12)
    all_came(gm_recv, 2)
    total = jnp.sum(gm_recv[...].astype(F32), axis=0)
    g_bc[...] = total[:8]
    m_bc[...] = total[8:]
    g_full[me] = total[:8]
    m_full[me] = total[8:]
    spread(g_bc, g_full, 3)
    for i in range(4, 7):
        ours(i)
    choose()
    for i in range(7, 9):
        ours(i)
    second(2, 0)
    second(2, 1)
    for i in range(9, 11):
        ours(i)
    all_came(g_full, 3)
    a_ref[...] = g_full[...].reshape(size, size) * (1.0 / slab_rows)
    between = {
        64: lambda: (ours(11), ours(12), second(1, 0), second(1, 1)),
        128: lambda: (ours(13), ours(14), second(3, 0), second(3, 1), spread(m_bc, m_full, 4)),
        192: lambda: (ours(15), assemble(), leave(0)),
    }
    for count in factor_steps(a_ref):
        if count in between:
            between[count]()
    leave(1)
    second(0, 0)
    second(0, 1)
    all_came(m_full, 4)
    mix_high, mix_low = split(m_full[...].reshape(size, size))
    prow = prow_ref[...]
    cross = x_v[...] - dot(mix_high, prow) - dot(mix_low, prow)
    column = lax.broadcasted_iota(jnp.int32, (size, size), 1)
    w_high, w_low = split(jnp.where(column <= row, a_ref[...], 0.0))
    c_high, c_low = split(cross)
    right = dot(w_high, c_high) + dot(w_high, c_low) + dot(w_low, c_high)
    right_out[...] = (right.T * (1.0 / math.sqrt(slab_rows))).astype(BF16)
    for copy in z_sends:
        copy.wait_recv()
    z_out[...] = z_r[...]
    for copy in waits:
        copy.wait_send()
    await_bytes(q_send.at[pl.ds(1, n - 1)], ar_ss.at[0])
    await_bytes(q_full.at[pl.ds(1, n - 1)], ar_ss.at[1])
    await_bytes(gm_send.at[pl.ds(1, n - 1)], ar_ss.at[2])
    await_bytes(g_full.at[pl.ds(1, n - 1)], ar_ss.at[3])
    await_bytes(m_full.at[pl.ds(1, n - 1)], ar_ss.at[4])
    await_bytes(a3.at[pl.ds(0, 2 * n - 2)], ar_ss.at[5])
    await_bytes(c1.at[pl.ds(0, n - 1)], ar_ss.at[6])


def fused_call(slab_rows, table, column, inverse, rows, row_map, trailing, sketch):
    length, cols = trailing.shape
    wide = rows.shape[1]
    vmem = pl.BlockSpec(memory_space=pltpu.VMEM)
    anyw = pl.BlockSpec(memory_space=pl.ANY)
    dma = pltpu.SemaphoreType.DMA

    def kernel(*refs):
        fused_kernel(slab_rows, *refs)

    return pl.pallas_call(
        kernel,
        out_shape=(
            jax.ShapeDtypeStruct((length, 256), BF16),
            jax.ShapeDtypeStruct((wide, 256), BF16),
            jax.ShapeDtypeStruct((2, 4, 256, 128), BF16),
        ),
        in_specs=[pl.BlockSpec(memory_space=pltpu.SMEM), vmem, vmem, vmem, vmem, anyw, anyw],
        out_specs=(vmem, vmem, vmem),
        scratch_shapes=[
            pltpu.VMEM((length, cols), BF16),
            pltpu.VMEM((cols, 256), BF16),
            pltpu.VMEM((wide, 256), BF16),
            pltpu.VMEM((length, 256), F32),
            pltpu.VMEM((256, length), BF16),
            pltpu.VMEM((32, 8, 256), F32),
            pltpu.VMEM((32, 8, 256), F32),
            pltpu.VMEM((8, 256), F32),
            pltpu.VMEM((32, 8, 256), F32),
            pltpu.VMEM((32, 16, 256), BF16),
            pltpu.VMEM((32, 16, 256), BF16),
            pltpu.VMEM((8, 256), F32),
            pltpu.VMEM((32, 8, 256), F32),
            pltpu.VMEM((8, 256), F32),
            pltpu.VMEM((32, 8, 256), F32),
            pltpu.VMEM((16, 256, wide), BF16),
            pltpu.VMEM((16, 256, wide), BF16),
            pltpu.VMEM((2, 12, 128, wide), BF16),
            pltpu.VMEM((2, 12, 128, wide), BF16),
            pltpu.VMEM((2, 4, 128, wide), F32),
            pltpu.VMEM((2, 2, 64, wide), BF16),
            pltpu.VMEM((2, 2, 64, wide), BF16),
            pltpu.VMEM((2, 2, 128, wide), BF16),
            pltpu.VMEM((2, 2, 128, wide), BF16),
            pltpu.VMEM((256, wide), F32),
            pltpu.VMEM((256, 256), F32),
            pltpu.VMEM((16, 2, 2, 16, 128), BF16),
            pltpu.VMEM((65, 16, 128), BF16),
            pltpu.VMEM((32, 4, 16, 128), BF16),
            pltpu.VMEM((16, 2, 4, 16, 128), BF16),
            pltpu.VMEM((1024, 256), BF16),
            pltpu.VMEM((2, 4, 256, 128), BF16),
            pltpu.VMEM((2, 4, 256, 128), BF16),
            dma((17,)),
            dma((7,)),
            dma((7,)),
            dma((16,)),
            dma((16,)),
            dma((2, 12)),
            dma((2, 12)),
            dma((2, 2)),
            dma((2, 2)),
            dma((2, 2)),
            dma((2, 2)),
            dma((2, 4)),
            dma((2, 4)),
        ],
        compiler_params=pltpu.CompilerParams(
            collective_id=0, has_side_effects=True, vmem_limit_bytes=VLIM
        ),
        name="fused",
    )(table, column, inverse, rows, row_map, trailing, sketch)


def write_kernel(l_ref, right_ref, z_ref, l_out, right_out, parent_out):
    l_out[...] = l_ref[...]
    right_out[...] = right_ref[...]
    for g in range(4):
        for h in range(2):
            at = g * 256 + 128 * h
            parent_out[:, at : at + 128] = z_ref[h, g]


def write_call(factored, right, parts):
    vmem = pl.BlockSpec(memory_space=pltpu.VMEM)
    return pl.pallas_call(
        write_kernel,
        out_shape=(
            jax.ShapeDtypeStruct(factored.shape, BF16),
            jax.ShapeDtypeStruct(right.shape, BF16),
            jax.ShapeDtypeStruct((256, 1024), BF16),
        ),
        in_specs=[vmem] * 3,
        out_specs=(vmem, vmem, vmem),
        name="write",
    )(factored, right, parts)


def slot_table(parent_block, parent_slot):
    front = lax.axis_index("front")
    blocks = lax.dynamic_slice(parent_block, (front, 0), (1, parent_block.shape[1]))[0]
    parents = jnp.arange(parent_slot.shape[0], dtype=jnp.int32)
    owners = jnp.sum(jnp.where(blocks[:, None] == parents[None, :], parent_slot[None, :], 0), axis=1)
    slot = jnp.arange(128, dtype=jnp.int32)
    device = slot % 4 * 32 + slot // 4
    j = jnp.arange(blocks.shape[0], dtype=jnp.int32)
    return 64 + jnp.sum(jnp.where(owners[None, :] == device[:, None], j[None, :] - 64, 0), axis=1)


def body(
    panel_column, upper_inverse, panel_rows, trailing, sketch, row_map, parent_block, parent_slot
):
    slab_rows = trailing.shape[1] * lax.axis_size("blk")
    results = fused_call(
        slab_rows,
        slot_table(parent_block, parent_slot),
        panel_column[0],
        upper_inverse[0],
        panel_rows[0],
        row_map[0],
        trailing[0],
        sketch,
    )
    factored, right, parent = write_call(*results)
    return factored[None], right[None], parent


def solution(mesh):
    return jax.shard_map(
        body,
        mesh=mesh,
        in_specs=(
            P("front", "blk", None),
            P("front", None, None),
            P("front", None, "blk"),
            P("front", "blk", None),
            P(),
            P("front", "blk", None),
            P(),
            P(),
        ),
        out_specs=(P("front", "blk", None), P("front", "blk", None), P(("front", "blk"), None)),
        check_vma=False,
    )
```

time: 327 us -> 77.4 us (0.24)
  waiting for transfers between devices: 194 us -> 0 us
  Pallas kernels: 0 us -> 74.4 us
  other arithmetic: 56.8 us -> 1.46 us
  matrix products: 48.3 us -> 0 us
  between operations: 15.3 us -> 0.67 us
  local copies, waits for them, and re-layouts: 7.4 us -> 0.68 us
  starting transfers between devices: 4.48 us -> 0 us
    all_gather x3 -> x0, waiting for transfers between devices: 146 us -> none  [the longest x1 58 us: body(): lax.all_gather(panel_rows, 'blk', axis=2, tiled=True)[0]]
    pallas_call x0 -> x2, Pallas kernels: none -> 74.4 us  [the longest x1 72.1 us: fused_call(): pl.pallas_call(kernel, out_shape=(jax.ShapeDtypeStruct((length, 256), BF1...]
    another operation x9 -> x0, other arithmetic: 53.7 us -> none  [the longest x6 34 us: gram_factor(): return jnp.linalg.cholesky(gram_matrix)]
    dot_general x7 -> x0, matrix products: 44.3 us -> none  [the longest x1 12.6 us: body(): lax.dot_general(window, sketched, (((0,), (0,)), ((), ())), preferred_ele...]
    reduce_scatter x1 -> x0, waiting for transfers between devices: 39.9 us -> none  [body(): lax.psum_scatter(lax.dot_general(window, sketched, (((0,), (0,)), ((), ()...]
    all_to_all x1 -> x0, waiting for transfers between devices: 7.27 us -> none  [body(): lax.all_to_all(outgoing, 'front', split_axis=1, concat_axis=1, tiled=True)]
    all_to_all x1 -> x0, starting transfers between devices: 4.14 us -> none  [body(): lax.all_to_all(outgoing, 'front', split_axis=1, concat_axis=1, tiled=True)]
    another operation x8 -> x0, matrix products: 4.07 us -> none  [the longest x3 2.28 us: body(): jax.scipy.linalg.solve_triangular(factor_low, cross_share.T, lower=True)]
  transfers between devices with their start and end apart: 5 -> 0, of which waited for: 5 -> 0; matrix products, arithmetic and copies ran while one was open for 25% -> 0% of each run, Pallas kernels for 0% -> 0%
where the time goes in v2:
time: 77.4 us; the launch traced here: 77.2 us
  Pallas kernels  74.4 us (96%)
  other arithmetic  1.46 us (2%)
    pallas_call x1, Pallas kernels, fused_call(): pl.pallas_call(kernel, out_shape=(jax.ShapeDtypeStruct((length, 256), BF1...  72.1 us
    pallas_call x1, Pallas kernels, write_call(): pl.pallas_call(write_kernel, out_shape=(jax.ShapeDtypeStruct(factored.sha...  2.28 us

profile of v2, /device:TPU:1, one launch (start us, length us, event | category | flops | bytes accessed | tf_op | source)
XLA Modules:
  0.0 77.2 jit_solution(3288867816602938999)
XLA Ops:
  0.6 0.0 copy-start
  0.6 0.7 copy-done
  1.3 0.8 %select_reduce_fusion.1 = s32[64]{0:T(128)S(1)} fusion(s32[96]{0:T(128)} %param.15, s32[64]{0:T(128)S(1)} %dynamic-slice_bitcast_fusion), kind=kLoop, calls=%fused_computation.1 | loop fusion | flops 18368 | bytes 896 | tf_op jit(solution)/shard_map/reduce_sum | solution.py:535
  2.2 0.1 select_reduce_fusion
  2.3 0.5 broadcast_add_fusion.refs_0_
  2.8 72.1 %fused.1 = (bf16[512,256]{1,0:T(8,128)(2,1)}, bf16[384,256]{1,0:T(8,128)(2,1)}, bf16[2,4,256,128]{3,2,1,0:T(8,128)(2,1)}) custom-call(s32[128]{0:T(128)} %broadcast_add_fusion.refs_0_, bf16[512,256]{1,0:T(8,128)(2,1)} %bitcast.10, bf16[256,256]{1,0:T(8,128)(2,1)} %bitcast.12, bf16[256,384]{1,0:T(8,128)(2,1)} %bitcast.11, s32[2,256]{1,0:T(2,128)} %bitcast.13, ...), custom_call_target="tpu_custom_call" | custom-call | tf_op jit(solution)/shard_map/fused/pallas_call | solution.py:443
  74.9 2.3 %write.1 = (bf16[512,256]{1,0:T(8,128)(2,1)}, bf16[384,256]{1,0:T(8,128)(2,1)}, bf16[256,1024]{1,0:T(8,128)(2,1)}) custom-call(bf16[512,256]{1,0:T(8,128)(2,1)} %get-tuple-element.9.l_ref, bf16[384,256]{1,0:T(8,128)(2,1)} %get-tuple-element.10.right_ref, bf16[2,4,256,128]{3,2,1,0:T(8,128)(2,1)} %get-tuple-element.11.z_ref), custom_call_target="tpu_custom_call" | custom-call | tf_op jit(solution)/shard_map/write/pallas_call | solution.py:518
  (3 shorter events, 0.0 us)
Async XLA Ops:
  0.6 0.7 copy-start

commit v3 on v2

--- a/solution.py
+++ b/solution.py
@@ -13,8 +13,8 @@
 VLIM = 62 * 1024 * 1024
 
 ORDER = (
-    (2, 2), (2, 0), (2, 1), (2, 3), (0, 2), (1, 2), (3, 2), (1, 1),
-    (3, 3), (1, 3), (3, 1), (1, 0), (0, 1), (3, 0), (0, 3), (0, 0),
+    (2, 2), (2, 0), (0, 2), (2, 1), (1, 2), (2, 3), (3, 2), (1, 3),
+    (3, 1), (3, 0), (0, 3), (1, 0), (0, 1), (1, 1), (3, 3), (0, 0),
 )
 
 
@@ -127,10 +127,11 @@
     table, col_ref, uinv_ref, prow_ref, map_ref, t_hbm, om_hbm,
     l_out, right_out, z_out,
     t_v, om_v, own_v, y_v, st_v,
-    q_send, q_recv, q_bc, q_full, gm_send, gm_recv, g_bc, g_full, m_bc, m_full,
+    q_send, q_pair, q_mid, q_recv, q_bc, q_full,
+    gm_send, gm_pair, gm_mid, gm_recv, g_bc, g_full, m_bc, m_full,
     pair_s, pair_r, s1_s, s1_r, acc, s2_s, s2_r, s3_s, s3_r, x_v, a_ref,
     a0, a3, c1, c4, big, z_s, z_r,
-    ld_sem, ar_ss, ar_rs, pair_ss, pair_rs, s1_ss, s1_rs, s2_ss, s2_rs, s3_ss, s3_rs,
+    ld_sem, ar_ss, ar_rs, swap_ss, swap_rs, pair_ss, pair_rs, s1_ss, s1_rs, s2_ss, s2_rs, s3_ss, s3_rs,
     z_ss, z_rs,
 ):
     me = lax.axis_index("blk")
@@ -170,22 +171,38 @@
             one.start()
         copies.append(pair)
 
+    chips = n // 2
+    mine = me // 2
+
     def scatter(src, dst, phase):
-        @pl.loop(1, n)
+        @pl.loop(1, chips)
         def _(i):
-            peer = lax.rem(me + i, n)
+            peer = lax.rem(mine + i, chips)
             remote(
-                src.at[peer], dst.at[i], ar_ss.at[phase], ar_rs.at[phase], {"blk": peer}
+                src.at[peer], dst.at[i], ar_ss.at[phase], ar_rs.at[phase], {"blk": peer * 2 + c}
             ).start()
 
+        dst[0] = src[mine]
+
     def spread(src, dst, phase):
-        @pl.loop(1, n)
+        @pl.loop(1, chips)
         def _(i):
-            peer = lax.rem(me + i, n)
-            remote(src, dst.at[me], ar_ss.at[phase], ar_rs.at[phase], {"blk": peer}).start()
+            peer = lax.rem(mine + i, chips)
+            remote(
+                src, dst.at[c, mine], ar_ss.at[phase], ar_rs.at[phase], {"blk": peer * 2 + c}
+            ).start()
+
+        dst[c, mine] = src[...]
 
     def all_came(dst, phase):
-        await_bytes(dst.at[pl.ds(1, n - 1)], ar_rs.at[phase])
+        await_bytes(dst.at[pl.ds(1, chips - 1)], ar_rs.at[phase])
+
+    def swap(i, src, dst):
+        return send(src, dst, swap_ss.at[i], swap_rs.at[i], partner)
+
+    def join(full, phase, i):
+        await_bytes(full.at[0, pl.ds(1, chips - 1)], ar_rs.at[phase])
+        return swap(i, full.at[c], full.at[c])
 
     def chip(dx, dy):
         return lax.rem(x + dx, 4) * 4 + lax.rem(y + dy, 4)
@@ -207,8 +224,7 @@
     factored = dot(col_ref[...], uinv_ref[...]).astype(BF16)
     l_out[...] = factored
     pl.semaphore_wait(barrier, n - 1 + fronts - 1)
-    scatter(q_send, q_recv, 0)
-    q_recv[0] = q_send[me]
+    other = swap(0, q_send.at[1 - c], q_pair)
 
     def sketch_step(k):
         for one in copies[k]:
@@ -220,26 +236,26 @@
         else:
             y_v[...] += out
 
-    for k in range(loads // 2):
+    sketch_step(0)
+    other.wait_recv()
+    q_mid[...] = q_send[c] + q_pair[...]
+    scatter(q_mid, q_recv, 0)
+    for k in range(1, 4):
         sketch_step(k)
     all_came(q_recv, 0)
-    total = jnp.sum(q_recv[...], axis=0)
-    q_bc[...] = total
-    q_full[me] = total
+    q_bc[...] = jnp.sum(q_recv[...], axis=0)
     spread(q_bc, q_full, 1)
-    for k in range(loads // 2, loads):
+    for k in range(4, loads):
         sketch_step(k)
-    all_came(q_full, 1)
+    join(q_full, 1, 1).wait_recv()
     q_high, q_low = split(q_full[...].reshape(size, size))
     sk32 = y_v[...] - dot(factored, q_high) - dot(factored, q_low)
     sk = sk32.astype(BF16)
     st_v[...] = sk32.T.astype(BF16)
     st = st_v[...]
-    gram = dot(st, sk).reshape(n, 8, size)
-    mix = dot(st, factored).reshape(n, 8, size)
-    gm_send[...] = jnp.concatenate([gram, mix], axis=1).astype(BF16)
-    scatter(gm_send, gm_recv, 2)
-    gm_recv[0] = gm_send[me]
+    gm_send[:, :, :8, :] = dot(st, sk).reshape(2, chips, 8, size)
+    gm_send[:, :, 8:, :] = dot(st, factored).reshape(2, chips, 8, size)
+    other = swap(2, gm_send.at[1 - c], gm_pair)
     row = lax.broadcasted_iota(jnp.int32, (size, size), 0)
     for k in range(2):
         pick = (map_ref[k : k + 1, :] == row).astype(BF16)
@@ -247,16 +263,17 @@
         for h in range(2):
             a0[:, h, k] = moved[:, 128 * h : 128 * h + 128].reshape(16, 16, 128)
 
-    @pl.loop(1, n)
-    def _(i):
-        peer = lax.rem(me + i, n)
-        remote(
-            a0.at[peer // 2, lax.rem(peer, 2)],
-            a3.at[pl.ds(2 * me, 2)],
-            ar_ss.at[5],
-            ar_rs.at[5],
-            {"blk": peer},
-        ).start()
+    def spill():
+        @pl.loop(1, n)
+        def _(i):
+            peer = lax.rem(me + i, n)
+            remote(
+                a0.at[peer // 2, lax.rem(peer, 2)],
+                a3.at[pl.ds(2 * me, 2)],
+                ar_ss.at[5],
+                ar_rs.at[5],
+                {"blk": peer},
+            ).start()
 
     a3[pl.ds(2 * me, 2)] = a0[me // 2, c]
     a3[2 * n] = jnp.zeros((16, 128), BF16)
@@ -374,43 +391,47 @@
             )
         z_r[h, front] = z_s[h, front]
 
-    for i in range(16):
+    theirs(0)
+    theirs(1)
+    other.wait_recv()
+    gm_mid[...] = (gm_send[c] + gm_pair[...]).astype(BF16)
+    scatter(gm_mid, gm_recv, 2)
+    spill()
+    for i in range(2, 16):
         theirs(i)
-        if i >= 12:
-            ours(i - 12)
+        if 4 <= i < 8:
+            ours(i - 4)
     all_came(gm_recv, 2)
     total = jnp.sum(gm_recv[...].astype(F32), axis=0)
     g_bc[...] = total[:8]
     m_bc[...] = total[8:]
-    g_full[me] = total[:8]
-    m_full[me] = total[8:]
     spread(g_bc, g_full, 3)
-    for i in range(4, 7):
+    for i in range(4, 11):
         ours(i)
     choose()
-    for i in range(7, 9):
-        ours(i)
     second(2, 0)
     second(2, 1)
-    for i in range(9, 11):
+    for i in range(11, 16):
         ours(i)
-    all_came(g_full, 3)
+    spread(m_bc, m_full, 4)
+    join(g_full, 3, 3).wait_recv()
     a_ref[...] = g_full[...].reshape(size, size) * (1.0 / slab_rows)
     between = {
-        64: lambda: (ours(11), ours(12), second(1, 0), second(1, 1)),
-        128: lambda: (ours(13), ours(14), second(3, 0), second(3, 1), spread(m_bc, m_full, 4)),
-        192: lambda: (ours(15), assemble(), leave(0)),
+        64: lambda: (second(1, 0), second(1, 1)),
+        128: lambda: (assemble(), leave(0)),
+        192: lambda: (second(3, 0), second(3, 1)),
     }
     for count in factor_steps(a_ref):
         if count in between:
             between[count]()
     leave(1)
+    join(m_full, 4, 4).wait_recv()
+    mix_high, mix_low = split(m_full[...].reshape(size, size))
+    prow = prow_ref[...]
+    taken = dot(mix_high, prow) + dot(mix_low, prow)
     second(0, 0)
     second(0, 1)
-    all_came(m_full, 4)
-    mix_high, mix_low = split(m_full[...].reshape(size, size))
-    prow = prow_ref[...]
-    cross = x_v[...] - dot(mix_high, prow) - dot(mix_low, prow)
+    cross = x_v[...] - taken
     column = lax.broadcasted_iota(jnp.int32, (size, size), 1)
     w_high, w_low = split(jnp.where(column <= row, a_ref[...], 0.0))
     c_high, c_low = split(cross)
@@ -421,11 +442,11 @@
     z_out[...] = z_r[...]
     for copy in waits:
         copy.wait_send()
-    await_bytes(q_send.at[pl.ds(1, n - 1)], ar_ss.at[0])
-    await_bytes(q_full.at[pl.ds(1, n - 1)], ar_ss.at[1])
-    await_bytes(gm_send.at[pl.ds(1, n - 1)], ar_ss.at[2])
-    await_bytes(g_full.at[pl.ds(1, n - 1)], ar_ss.at[3])
-    await_bytes(m_full.at[pl.ds(1, n - 1)], ar_ss.at[4])
+    await_bytes(q_mid.at[pl.ds(1, chips - 1)], ar_ss.at[0])
+    await_bytes(q_mid.at[pl.ds(1, chips - 1)], ar_ss.at[1])
+    await_bytes(gm_mid.at[pl.ds(1, chips - 1)], ar_ss.at[2])
+    await_bytes(q_mid.at[pl.ds(1, chips - 1)], ar_ss.at[3])
+    await_bytes(q_mid.at[pl.ds(1, chips - 1)], ar_ss.at[4])
     await_bytes(a3.at[pl.ds(0, 2 * n - 2)], ar_ss.at[5])
     await_bytes(c1.at[pl.ds(0, n - 1)], ar_ss.at[6])
 
@@ -455,16 +476,20 @@
             pltpu.VMEM((wide, 256), BF16),
             pltpu.VMEM((length, 256), F32),
             pltpu.VMEM((256, length), BF16),
-            pltpu.VMEM((32, 8, 256), F32),
-            pltpu.VMEM((32, 8, 256), F32),
+            pltpu.VMEM((2, 16, 8, 256), F32),
+            pltpu.VMEM((16, 8, 256), F32),
+            pltpu.VMEM((16, 8, 256), F32),
+            pltpu.VMEM((16, 8, 256), F32),
             pltpu.VMEM((8, 256), F32),
-            pltpu.VMEM((32, 8, 256), F32),
-            pltpu.VMEM((32, 16, 256), BF16),
-            pltpu.VMEM((32, 16, 256), BF16),
+            pltpu.VMEM((2, 16, 8, 256), F32),
+            pltpu.VMEM((2, 16, 16, 256), F32),
+            pltpu.VMEM((16, 16, 256), F32),
+            pltpu.VMEM((16, 16, 256), BF16),
+            pltpu.VMEM((16, 16, 256), BF16),
             pltpu.VMEM((8, 256), F32),
-            pltpu.VMEM((32, 8, 256), F32),
+            pltpu.VMEM((2, 16, 8, 256), F32),
             pltpu.VMEM((8, 256), F32),
-            pltpu.VMEM((32, 8, 256), F32),
+            pltpu.VMEM((2, 16, 8, 256), F32),
             pltpu.VMEM((16, 256, wide), BF16),
             pltpu.VMEM((16, 256, wide), BF16),
             pltpu.VMEM((2, 12, 128, wide), BF16),
@@ -486,6 +511,8 @@
             dma((17,)),
             dma((7,)),
             dma((7,)),
+            dma((5,)),
+            dma((5,)),
             dma((16,)),
             dma((16,)),
             dma((2, 12)),

time: 77.4 us -> 72.7 us (0.939)
  Pallas kernels: 74.4 us -> 69.7 us
    pallas_call x1, Pallas kernels: 72.1 us -> 67.4 us  [fused_call(): pl.pallas_call(kernel, out_shape=(jax.ShapeDtypeStruct((length, 256), BF1...]
where the time goes in v3:
time: 72.7 us; the launch traced here: 72.5 us
  Pallas kernels  69.7 us (96%)
  other arithmetic  1.46 us (2%)
    pallas_call x1, Pallas kernels, fused_call(): pl.pallas_call(kernel, out_shape=(jax.ShapeDtypeStruct((length, 256), BF1...  67.4 us
    pallas_call x1, Pallas kernels, write_call(): pl.pallas_call(write_kernel, out_shape=(jax.ShapeDtypeStruct(factored.sha...  2.28 us

profile of v3, /device:TPU:1, one launch (start us, length us, event | category | flops | bytes accessed | tf_op | source)
XLA Modules:
  0.0 72.5 jit_solution(7620230164901253930)
XLA Ops:
  0.6 0.0 copy-start
  0.6 0.7 copy-done
  1.3 0.8 %select_reduce_fusion.1 = s32[64]{0:T(128)S(1)} fusion(s32[96]{0:T(128)} %param.15, s32[64]{0:T(128)S(1)} %dynamic-slice_bitcast_fusion), kind=kLoop, calls=%fused_computation.1 | loop fusion | flops 18368 | bytes 896 | tf_op jit(solution)/shard_map/reduce_sum | solution.py:562
  2.2 0.1 select_reduce_fusion
  2.3 0.5 broadcast_add_fusion.refs_0_
  2.8 67.4 %fused.1 = (bf16[512,256]{1,0:T(8,128)(2,1)}, bf16[384,256]{1,0:T(8,128)(2,1)}, bf16[2,4,256,128]{3,2,1,0:T(8,128)(2,1)}) custom-call(s32[128]{0:T(128)} %broadcast_add_fusion.refs_0_, bf16[512,256]{1,0:T(8,128)(2,1)} %bitcast.10, bf16[256,256]{1,0:T(8,128)(2,1)} %bitcast.12, bf16[256,384]{1,0:T(8,128)(2,1)} %bitcast.11, s32[2,256]{1,0:T(2,128)} %bitcast.13, ...), custom_call_target="tpu_custom_call" | custom-call | tf_op jit(solution)/shard_map/fused/pallas_call | solution.py:464
  70.2 2.3 %write.1 = (bf16[512,256]{1,0:T(8,128)(2,1)}, bf16[384,256]{1,0:T(8,128)(2,1)}, bf16[256,1024]{1,0:T(8,128)(2,1)}) custom-call(bf16[512,256]{1,0:T(8,128)(2,1)} %get-tuple-element.9.l_ref, bf16[384,256]{1,0:T(8,128)(2,1)} %get-tuple-element.10.right_ref, bf16[2,4,256,128]{3,2,1,0:T(8,128)(2,1)} %get-tuple-element.11.z_ref), custom_call_target="tpu_custom_call" | custom-call | tf_op jit(solution)/shard_map/write/pallas_call | solution.py:545
  (3 shorter events, 0.0 us)
Async XLA Ops:
  0.6 0.7 copy-start

commit v4 on v3

--- a/solution.py
+++ b/solution.py
@@ -40,6 +40,25 @@
 
 def await_bytes(ref, sem):
     pltpu.make_async_copy(ref, ref, sem).wait()
+
+
+def as_column(line):
+    k = line.shape[1]
+    rows = lax.broadcasted_iota(jnp.int32, (k, k), 0)
+    same = rows == lax.broadcasted_iota(jnp.int32, (k, k), 1)
+    return jnp.sum(jnp.where(same, line, 0), axis=1, keepdims=True)
+
+
+def slot_table(blocks, slots):
+    count, parents = blocks.shape[1], slots.shape[1]
+    number = lax.broadcasted_iota(jnp.int32, (parents, count), 0)
+    hit = number == blocks
+    owners = jnp.sum(jnp.where(hit, as_column(slots), 0), axis=0, keepdims=True)
+    slot = lax.broadcasted_iota(jnp.int32, (count, 128), 1)
+    device = slot % 4 * 32 + slot // 4
+    j = lax.broadcasted_iota(jnp.int32, (count, 128), 0)
+    goes = as_column(owners) == device
+    return jnp.min(jnp.where(goes, j, count), axis=0, keepdims=True)
 
 
 def factor_steps(a_ref, block=64, width=8, every=16):
@@ -124,7 +143,7 @@
 
 def fused_kernel(
     slab_rows,
-    table, col_ref, uinv_ref, prow_ref, map_ref, t_hbm, om_hbm,
+    pb_ref, slot_ref, col_ref, uinv_ref, prow_ref, map_ref, t_hbm, om_hbm,
     l_out, right_out, z_out,
     t_v, om_v, own_v, y_v, st_v,
     q_send, q_pair, q_mid, q_recv, q_bc, q_full,
@@ -132,7 +151,7 @@
     pair_s, pair_r, s1_s, s1_r, acc, s2_s, s2_r, s3_s, s3_r, x_v, a_ref,
     a0, a3, c1, c4, big, z_s, z_r,
     ld_sem, ar_ss, ar_rs, swap_ss, swap_rs, pair_ss, pair_rs, s1_ss, s1_rs, s2_ss, s2_rs, s3_ss, s3_rs,
-    z_ss, z_rs,
+    z_ss, z_rs, table_v, table, table_sem,
 ):
     me = lax.axis_index("blk")
     front = lax.axis_index("front")
@@ -219,6 +238,9 @@
         waits.append(copy)
         return copy
 
+    table_v[...] = slot_table(pb_ref[pl.ds(front, 1), :], slot_ref[...])
+    table_copy = pltpu.make_async_copy(table_v, table, table_sem)
+    table_copy.start()
     own_copy.wait()
     q_send[...] = dot(prow_ref[...], own_v[...]).reshape(q_send.shape)
     factored = dot(col_ref[...], uinv_ref[...]).astype(BF16)
@@ -280,11 +302,12 @@
 
     def choose():
         await_bytes(a3.at[pl.ds(0, 2 * n - 2)], ar_rs.at[5])
+        table_copy.wait()
 
         @pl.loop(0, n)
         def _(t):
             for g in range(fronts):
-                c1[t, g] = a3[table[t * fronts + g]]
+                c1[t, g] = a3[table[0, t * fronts + g]]
 
         @pl.loop(1, n)
         def _(i):
@@ -406,9 +429,11 @@
     g_bc[...] = total[:8]
     m_bc[...] = total[8:]
     spread(g_bc, g_full, 3)
-    for i in range(4, 11):
+    for i in range(4, 8):
         ours(i)
     choose()
+    for i in range(8, 11):
+        ours(i)
     second(2, 0)
     second(2, 1)
     for i in range(11, 16):
@@ -451,7 +476,7 @@
     await_bytes(c1.at[pl.ds(0, n - 1)], ar_ss.at[6])
 
 
-def fused_call(slab_rows, table, column, inverse, rows, row_map, trailing, sketch):
+def fused_call(slab_rows, blocks, slots, column, inverse, rows, row_map, trailing, sketch):
     length, cols = trailing.shape
     wide = rows.shape[1]
     vmem = pl.BlockSpec(memory_space=pltpu.VMEM)
@@ -468,7 +493,7 @@
             jax.ShapeDtypeStruct((wide, 256), BF16),
             jax.ShapeDtypeStruct((2, 4, 256, 128), BF16),
         ),
-        in_specs=[pl.BlockSpec(memory_space=pltpu.SMEM), vmem, vmem, vmem, vmem, anyw, anyw],
+        in_specs=[vmem] * 6 + [anyw, anyw],
         out_specs=(vmem, vmem, vmem),
         scratch_shapes=[
             pltpu.VMEM((length, cols), BF16),
@@ -523,25 +548,38 @@
             dma((2, 2)),
             dma((2, 4)),
             dma((2, 4)),
+            pltpu.VMEM((1, 128), jnp.int32),
+            pltpu.SMEM((1, 128), jnp.int32),
+            dma(()),
         ],
         compiler_params=pltpu.CompilerParams(
             collective_id=0, has_side_effects=True, vmem_limit_bytes=VLIM
         ),
         name="fused",
-    )(table, column, inverse, rows, row_map, trailing, sketch)
-
-
-def write_kernel(l_ref, right_ref, z_ref, l_out, right_out, parent_out):
-    l_out[...] = l_ref[...]
-    right_out[...] = right_ref[...]
-    for g in range(4):
-        for h in range(2):
-            at = g * 256 + 128 * h
-            parent_out[:, at : at + 128] = z_ref[h, g]
+    )(blocks, slots, column, inverse, rows, row_map, trailing, sketch)
+
+
+def write_kernel(l_ref, right_ref, z_ref, l_out, right_out, parent_out, l_v, right_v, z_v, in_sem, out_sem):
+    routes = [(z_ref.at[h, g], z_v.at[h, g], (h, g)) for g in range(4) for h in range(2)]
+    reads = [(z, v, parent_out.at[:, pl.ds(g * 256 + 128 * h, 128)]) for z, v, (h, g) in routes]
+    reads += [(l_ref, l_v, l_out), (right_ref, right_v, right_out)]
+    inward = [
+        pltpu.make_async_copy(src, mid, in_sem.at[k]) for k, (src, mid, _) in enumerate(reads)
+    ]
+    outward = [
+        pltpu.make_async_copy(mid, dst, out_sem.at[k]) for k, (_, mid, dst) in enumerate(reads)
+    ]
+    for copy in inward:
+        copy.start()
+    for came, copy in zip(inward, outward):
+        came.wait()
+        copy.start()
+    for copy in outward:
+        copy.wait()
 
 
 def write_call(factored, right, parts):
-    vmem = pl.BlockSpec(memory_space=pltpu.VMEM)
+    anyw = pl.BlockSpec(memory_space=pl.ANY)
     return pl.pallas_call(
         write_kernel,
         out_shape=(
@@ -549,21 +587,17 @@
             jax.ShapeDtypeStruct(right.shape, BF16),
             jax.ShapeDtypeStruct((256, 1024), BF16),
         ),
-        in_specs=[vmem] * 3,
-        out_specs=(vmem, vmem, vmem),
+        in_specs=[anyw] * 3,
+        out_specs=(anyw, anyw, anyw),
+        scratch_shapes=[
+            pltpu.VMEM(factored.shape, BF16),
+            pltpu.VMEM(right.shape, BF16),
+            pltpu.VMEM(parts.shape, BF16),
+            pltpu.SemaphoreType.DMA((10,)),
+            pltpu.SemaphoreType.DMA((10,)),
+        ],
         name="write",
     )(factored, right, parts)
-
-
-def slot_table(parent_block, parent_slot):
-    front = lax.axis_index("front")
-    blocks = lax.dynamic_slice(parent_block, (front, 0), (1, parent_block.shape[1]))[0]
-    parents = jnp.arange(parent_slot.shape[0], dtype=jnp.int32)
-    owners = jnp.sum(jnp.where(blocks[:, None] == parents[None, :], parent_slot[None, :], 0), axis=1)
-    slot = jnp.arange(128, dtype=jnp.int32)
-    device = slot % 4 * 32 + slot // 4
-    j = jnp.arange(blocks.shape[0], dtype=jnp.int32)
-    return 64 + jnp.sum(jnp.where(owners[None, :] == device[:, None], j[None, :] - 64, 0), axis=1)
 
 
 def body(
@@ -572,7 +606,8 @@
     slab_rows = trailing.shape[1] * lax.axis_size("blk")
     results = fused_call(
         slab_rows,
-        slot_table(parent_block, parent_slot),
+        parent_block,
+        parent_slot[None],
         panel_column[0],
         upper_inverse[0],
         panel_rows[0],

time: 72.7 us -> 70.2 us (0.966)
  other arithmetic: 1.46 us -> 0 us
    reduce_sum x2 -> x0, other arithmetic: 0.93 us -> none  [the longest x1 0.83 us: slot_table(): jnp.sum(jnp.where(blocks[:, None] == parents[None, :], parent_slot[None,...]
where the time goes in v4:
time: 70.2 us; the launch traced here: 70 us
  Pallas kernels  69.2 us (99%)
  between operations  0.8 us (1%)
    pallas_call x1, Pallas kernels, fused_call(): pl.pallas_call(kernel, out_shape=(jax.ShapeDtypeStruct((length, 256), BF1...  67.1 us
    pallas_call x1, Pallas kernels, write_call(): pl.pallas_call(write_kernel, out_shape=(jax.ShapeDtypeStruct(factored.sha...  2.16 us

profile of v4, /device:TPU:1, one launch (start us, length us, event | category | flops | bytes accessed | tf_op | source)
XLA Modules:
  0.0 70.0 jit_solution(3458493155456815191)
XLA Ops:
  0.6 67.1 %fused.1 = (bf16[512,256]{1,0:T(8,128)(2,1)}, bf16[384,256]{1,0:T(8,128)(2,1)}, bf16[2,4,256,128]{3,2,1,0:T(8,128)(2,1)}) custom-call(s32[4,64]{1,0:T(4,128)} %refs_0_.1, s32[1,96]{1,0:T(1,128)} %bitcast.13, bf16[512,256]{1,0:T(8,128)(2,1)} %bitcast.9, bf16[256,256]{1,0:T(8,128)(2,1)} %bitcast.11, bf16[256,384]{1,0:T(8,128)(2,1)} %bitcast.10, ...), custom_call_target="tpu_custom_call" | custom-call | tf_op jit(solution)/shard_map/fused/pallas_call | solution.py:489
  67.7 2.2 %write.1 = (bf16[512,256]{1,0:T(8,128)(2,1)}, bf16[384,256]{1,0:T(8,128)(2,1)}, bf16[256,1024]{1,0:T(8,128)(2,1)}) custom-call(bf16[512,256]{1,0:T(8,128)(2,1)} %get-tuple-element.9.l_ref, bf16[384,256]{1,0:T(8,128)(2,1)} %get-tuple-element.10.right_ref, bf16[2,4,256,128]{3,2,1,0:T(8,128)(2,1)} %get-tuple-element.11.z_ref), custom_call_target="tpu_custom_call" | custom-call | tf_op jit(solution)/shard_map/write/pallas_call | solution.py:583

commit v5 on v4

--- a/solution.py
+++ b/solution.py
@@ -444,16 +444,20 @@
     between = {
         64: lambda: (second(1, 0), second(1, 1)),
         128: lambda: (assemble(), leave(0)),
-        192: lambda: (second(3, 0), second(3, 1)),
+        192: lambda: (second(3, 0), second(3, 1), joins.append(join(m_full, 4, 4))),
     }
+    joins = []
     for count in factor_steps(a_ref):
         if count in between:
             between[count]()
     leave(1)
-    join(m_full, 4, 4).wait_recv()
+    joins[0].wait_recv()
     mix_high, mix_low = split(m_full[...].reshape(size, size))
     prow = prow_ref[...]
     taken = dot(mix_high, prow) + dot(mix_low, prow)
+    for copy in z_sends[:3]:
+        copy.wait_recv()
+    z_out[0] = z_r[0]
     second(0, 0)
     second(0, 1)
     cross = x_v[...] - taken
@@ -462,9 +466,9 @@
     c_high, c_low = split(cross)
     right = dot(w_high, c_high) + dot(w_high, c_low) + dot(w_low, c_high)
     right_out[...] = (right.T * (1.0 / math.sqrt(slab_rows))).astype(BF16)
-    for copy in z_sends:
+    for copy in z_sends[3:]:
         copy.wait_recv()
-    z_out[...] = z_r[...]
+    z_out[1] = z_r[1]
     for copy in waits:
         copy.wait_send()
     await_bytes(q_mid.at[pl.ds(1, chips - 1)], ar_ss.at[0])

time: 70.2 us -> 70.2 us (level)
  no operation moved by 1% of the time
where the time goes in v5:
time: 70.2 us; the launch traced here: 70 us
  Pallas kernels  69.2 us (99%)
  between operations  0.8 us (1%)
    pallas_call x1, Pallas kernels, fused_call(): pl.pallas_call(kernel, out_shape=(jax.ShapeDtypeStruct((length, 256), BF1...  67.1 us
    pallas_call x1, Pallas kernels, write_call(): pl.pallas_call(write_kernel, out_shape=(jax.ShapeDtypeStruct(factored.sha...  2.16 us

profile of v5, /device:TPU:1, one launch (start us, length us, event | category | flops | bytes accessed | tf_op | source)
XLA Modules:
  0.0 70.0 jit_solution(17104649200191398317)
XLA Ops:
  0.6 67.1 %fused.1 = (bf16[512,256]{1,0:T(8,128)(2,1)}, bf16[384,256]{1,0:T(8,128)(2,1)}, bf16[2,4,256,128]{3,2,1,0:T(8,128)(2,1)}) custom-call(s32[4,64]{1,0:T(4,128)} %refs_0_.1, s32[1,96]{1,0:T(1,128)} %bitcast.13, bf16[512,256]{1,0:T(8,128)(2,1)} %bitcast.9, bf16[256,256]{1,0:T(8,128)(2,1)} %bitcast.11, bf16[256,384]{1,0:T(8,128)(2,1)} %bitcast.10, ...), custom_call_target="tpu_custom_call" | custom-call | tf_op jit(solution)/shard_map/fused/pallas_call | solution.py:493
  67.7 2.2 %write.1 = (bf16[512,256]{1,0:T(8,128)(2,1)}, bf16[384,256]{1,0:T(8,128)(2,1)}, bf16[256,1024]{1,0:T(8,128)(2,1)}) custom-call(bf16[512,256]{1,0:T(8,128)(2,1)} %get-tuple-element.9.l_ref, bf16[384,256]{1,0:T(8,128)(2,1)} %get-tuple-element.10.right_ref, bf16[2,4,256,128]{3,2,1,0:T(8,128)(2,1)} %get-tuple-element.11.z_ref), custom_call_target="tpu_custom_call" | custom-call | tf_op jit(solution)/shard_map/write/pallas_call | solution.py:587
